TPU v7x, 128 devices: a whole 4x4x4 slice. The times are simulated.
128 devices in a mesh: row: 8 (over y, core), grid: 16 (over z, x).
Axes of the slice: x: 4, y: 4, z: 4, core: 2. Of those that a mesh axis runs over, the one named last changes fastest.
Arguments:
- h_rows: bfloat16 [16, 2048, 2048], P('grid', 'row'), may hold values from -6 to 6
- x_blocks: bfloat16 [16, 16, 8, 128, 128], P('grid', 'row'), may hold values from -0.1875 to 0.1875
- x_cols: int32 [16, 16, 8], P('grid', 'row'), may hold values from 0 to 15
- sub_blocks: int32 [8, 16, 3, 6], P('row', 'grid'), may hold values from 0 to 15, as said below
- owners: int32 [8, 16, 3], P('row'), may hold values from 0 to 15, as said below
- shift_mu: float32 [1], replicated, may hold values from -4 to 4
- orbitals: bfloat16 [8, 16, 6, 768, 1536], P('row', 'grid'), may hold values from -0.125 to 0.125
Outputs:
- density: float32 [16, 1024], P('grid', 'row')
Inputs may be any that keep to these rules, and one draw needn't show every extreme that they name: `x_cols`: entries of a block row may repeat; repeated blocks add. `sub_blocks`: the 6 blocks of a submatrix are distinct; the first is its central block. Within each row index, a device's 3 submatrices go to distinct owners, and every owner receives 1 to 6 submatrices.
All inputs are finite; a program needn't handle non-finite values.
Results may differ from a plain program's by a relative error of at most 0.0003.
Values may be sent and summed in bfloat16 or wider, within the bound.
A program may use at most 128 MiB of HBM per device.

v0:
```python
import jax
import jax.numpy as jnp
from jax import lax
from jax.sharding import PartitionSpec as P

BLK = 128
OWN_MAX = 6
PLANE = 256
DEPTH = 4
MARG = 1
ORDER = 768


def from_behind(value, axis, steps):
    count = lax.axis_size(axis)
    pairs = [(source, (source + steps) % count) for source in range(count)]
    return lax.ppermute(value, axis, pairs)


def cut_along(value, dim, devices):
    before, after = (value.shape[:dim], value.shape[dim + 1 :])
    return jnp.moveaxis(value.reshape(*before, devices, -1, *after), dim, 0)


def sum_at_owner(value, axis, dim):
    parts = cut_along(value, dim, lax.axis_size(axis))
    arrived = lax.all_to_all(parts, axis, split_axis=0, concat_axis=0, tiled=True)
    return arrived.sum(axis=0)


def densify(blocks, cols, count):
    onehot = (cols[:, :, None] == jnp.arange(count, dtype=jnp.int32)[None, None, :]).astype(
        jnp.bfloat16
    )
    dense = jnp.einsum("rzk,rzab->rakb", onehot, blocks, preferred_element_type=jnp.float32)
    return dense.reshape(blocks.shape[0] * blocks.shape[2], count * blocks.shape[2]).astype(
        jnp.bfloat16
    )


def sign_batch(mats, potential):
    eye = jnp.eye(ORDER, dtype=jnp.float32)
    shifted = mats.astype(jnp.float32) - potential * eye[None]
    scale = jnp.sqrt(jnp.sum(shifted * shifted, axis=(1, 2)) / ORDER + 1e-06)
    first = (shifted / (2.0 * scale)[:, None, None]).astype(jnp.bfloat16)
    square = jnp.einsum("sij,sjk->sik", first, first, preferred_element_type=jnp.float32)
    helper = (3.0 * eye[None] - square).astype(jnp.bfloat16)
    second = (
        0.5 * jnp.einsum("sij,sjk->sik", first, helper, preferred_element_type=jnp.float32)
    ).astype(jnp.bfloat16)
    square_cols = jnp.einsum(
        "sij,sjk->sik", second, second[:, :, :BLK], preferred_element_type=jnp.float32
    )
    helper_cols = (3.0 * eye[None, :, :BLK] - square_cols).astype(jnp.bfloat16)
    last = 0.5 * jnp.einsum("sij,sjk->sik", second, helper_cols, preferred_element_type=jnp.float32)
    return (0.5 * (eye[None, :, :BLK] - last)).astype(jnp.bfloat16)


def on_device(h_rows, x_blocks, x_cols, sub_blocks, owners, shift_mu, orbitals):
    potential = shift_mu[0]
    nreg = h_rows.shape[2]
    count = nreg // BLK
    dense = densify(x_blocks[0], x_cols[0], count)
    product = jnp.dot(
        dense,
        lax.all_gather(h_rows, "row", axis=1, tiled=True)[0],
        preferred_element_type=jnp.float32,
    )
    whole = lax.all_gather(product.astype(jnp.bfloat16), "row", axis=0, tiled=True)
    blocks4 = whole.reshape(count, BLK, count, BLK)

    def extract(picks):
        rows = jnp.take(blocks4, picks, axis=0)
        return jnp.take(rows, picks, axis=2).reshape(ORDER, ORDER)

    mats = jax.vmap(extract)(sub_blocks[0, 0])
    built = sign_batch(mats, potential)
    ngrid = lax.axis_size("grid")
    myself = lax.axis_index("grid")
    table = owners[0]
    targets = lax.dynamic_index_in_dim(table, myself, 0, keepdims=False)
    hit = table == myself
    has = jnp.any(hit, axis=1)
    place = jnp.cumsum(has.astype(jnp.int32)) - 1
    select = has[None, :] & (place[None, :] == jnp.arange(OWN_MAX, dtype=jnp.int32)[:, None])
    selint = select.astype(jnp.int32)
    source = jnp.sum(selint * jnp.arange(ngrid, dtype=jnp.int32)[None, :], axis=1)
    live = jnp.any(select, axis=1)
    outgoing = jnp.zeros((ngrid, ORDER, BLK), jnp.bfloat16).at[targets].set(built)
    incoming = lax.all_to_all(outgoing, "grid", split_axis=0, concat_axis=0, tiled=True)
    columns = jnp.take(incoming, source, axis=0)
    phi = orbitals[0, 0]
    proj = jnp.einsum("tnm,tnx->tmx", columns, phi, preferred_element_type=jnp.float32)
    values = jnp.sum(proj * phi[:, :BLK, :].astype(jnp.float32), axis=1)
    window = jnp.sum(jnp.where(live[:, None], values, 0.0), axis=0).reshape(DEPTH + 2 * MARG, PLANE)
    core = window[MARG : MARG + DEPTH]
    from_prev = from_behind(window[MARG + DEPTH :], "grid", 1)
    from_next = from_behind(window[:MARG], "grid", -1)
    core = core.at[:MARG].add(from_prev)
    core = core.at[DEPTH - MARG :].add(from_next)
    return sum_at_owner(core.reshape(1, DEPTH * PLANE), "row", 1)


def solution(mesh):
    in_specs = (
        P("grid", "row", None),
        P("grid", "row", None, None, None),
        P("grid", "row", None),
        P("row", "grid", None, None),
        P("row", None, None),
        P(),
        P("row", "grid", None, None, None),
    )
    out_specs = P("grid", "row")
    return jax.shard_map(
        on_device, mesh=mesh, in_specs=in_specs, out_specs=out_specs, check_vma=False
    )
```

profile of v0, /device:TPU:1, one launch (start us, length us, event | category | flops | bytes accessed | tf_op | source)
XLA Modules:
  0.0 286.0 jit_solution(15188846171057671028)
XLA Ops:
  6.5 0.7 all-gather.3.cloned.1.call-update
  7.3 0.3 copy-done
  7.6 1.3 convolution_convert_fusion
  8.9 53.6 %all-gather.3.cloned.1.call-done = bf16[1,2048,2048]{2,1,0:T(8,128)(2,1)} async-done(((bf16[1,256,2048]{2,1,0:T(8,128)(2,1)}), bf16[1,2048,2048]{2,1,0:T(8,128)(2,1)}) %all-gather.3.cloned.1.call-update) | async-done | bytes 8388624 | tf_op jit(solution)/shard_map/all_gather | solution.py:66
  62.5 6.8 %fusion.4 = bf16[256,2048]{1,0:T(8,128)(2,1)} fusion(bf16[1,2048,2048]{2,1,0:T(8,128)(2,1)} %all-gather.3.cloned.1.call-done, bf16[32,8,16,128]{3,2,1,0:T(8,128)(2,1)S(1)} %bitcast.67), kind=kOutput, calls=%fused_computation.14 | convolution fusion | flops 2148007936 | bytes 10485760 | tf_op jit(solution)/shard_map/dot_general | solution.py:64
  70.3 0.2 dynamic-slice_reduce_fusion
  70.7 0.5 fusion.29
  71.2 2.5 fusion.13
  73.7 0.8 slice_convert_fusion
  74.5 0.8 slice_select_fusion
  75.3 1.8 compare_select_fusion
  77.1 42.2 %all-gather.5.cloned.1.call-done = bf16[2048,2048]{1,0:T(8,128)(2,1)} async-done(((bf16[256,2048]{1,0:T(8,128)(2,1)}), bf16[2048,2048]{1,0:T(8,128)(2,1)}) %all-gather.5.cloned.1.call-update) | async-done | bytes 8388624 | tf_op jit(solution)/shard_map/all_gather | solution.py:69
  119.4 9.8 %copy.30 = bf16[256,8,16,128]{3,2,1,0:T(8,128)(2,1)} copy(bf16[256,8,16,128]{3,1,2,0:T(8,128)(2,1)} %bitcast.66) | data formatting | bytes 16777216
  129.2 8.7 %gather_fusion = bf16[18,128,16,128]{3,2,1,0:T(8,128)(2,1)} fusion(bf16[16,128,16,128]{3,2,1,0:T(8,128)(2,1)} %bitcast.64, s32[1024]{0:T(1024)S(1)} %pad_clamp_fusion.1), kind=kCustom, calls=%fused_computation | custom fusion | bytes 18874440 | tf_op jit(solution)/shard_map/vmap(jit(_take))/gather | solution.py:73
  138.0 10.2 %copy.22 = bf16[18,128,16,128]{3,1,2,0:T(8,128)(2,1)} copy(bf16[18,128,16,128]{3,2,1,0:T(8,128)(2,1)} %gather_fusion) | data formatting | bytes 18874368 | tf_op jit(solution)/shard_map/vmap(jit(_take))/gather | solution.py:73
  148.1 8.3 %broadcast_select_fusion = bf16[3,6,128,16,128]{4,2,3,1,0:T(8,128)(2,1)} fusion(bf16[3,6,128,16,128]{4,2,3,1,0:T(8,128)(2,1)} %bitcast.65, pred[3,6]{1,0:T(4,128)(4,1)S(1)} %compare_and_fusion), kind=kLoop, calls=%fused_computation.4 | loop fusion | flops 4718592 | bytes 18874386 | tf_op jit(solution)/shard_map/vmap(jit(_take))/select_n | solution.py:73
  156.4 5.1 %gather_fusion.2 = bf16[18,6,128,128]{3,2,1,0:T(8,128)(2,1)S(1)} fusion(bf16[3,6,128,16,128]{4,2,3,1,0:T(8,128)(2,1)} %broadcast_select_fusion, s32[18]{0:T(128)S(1)} %reshape.241), kind=kCustom, calls=%fused_computation.2 | custom fusion | bytes 7078032 | tf_op jit(solution)/shard_map/vmap(jit(_take))/gather | solution.py:74
  161.5 5.2 %copy.23 = bf16[3,6,128,6,128]{4,3,2,1,0:T(8,128)(2,1)} copy(bf16[3,6,128,6,128]{4,2,1,3,0:T(8,128)(2,1)S(1)} %bitcast.62) | data formatting | bytes 7077888 | tf_op jit(solution)/shard_map/vmap(jit(_take))/gather | solution.py:74
  166.7 1.7 multiply_reduce_fusion
  168.4 7.2 %gather.16 = bf16[3,768,768]{2,1,0:T(8,128)(2,1)S(1)} reshape(bf16[3,6,128,6,128]{4,3,2,1,0:T(8,128)(2,1)} %copy.23) | data formatting | bytes 7077888 | tf_op jit(solution)/shard_map/vmap(jit(_take))/gather | solution.py:74
  175.6 12.1 %multiply_convert_fusion = bf16[3,768,768]{2,1,0:T(8,128)(2,1)} fusion(f32[768,768]{1,0:T(8,128)} %get-tuple-element.34, f32[3]{0:T(128)S(1)} %sqrt_multiply_fusion, f32[768,768]{1,0:T(8,128)} %get-tuple-element.35, bf16[3,768,768]{2,1,0:T(8,128)(2,1)S(1)} %gather.16, pred[3,768]{1,0:T(4,128)(4,1)S(1)} %bitcast.69), kind=kOutput, calls=%fused_computation.7 | convolution fusion | flops 5460590592 | bytes 11798796 | tf_op jit(solution)/shard_map/sij,sjk->sik/dot_general | solution.py:49
  187.7 5.4 %fusion.12 = bf16[3,768,128]{2,1,0:T(8,128)(2,1)S(1)} fusion(bf16[3,768,768]{2,1,0:T(8,128)(2,1)} %multiply_convert_fusion, f32[768,128]{1,0:T(8,128)} %slice_select_fusion, f32[768,128]{1,0:T(8,128)} %slice_convert_fusion), kind=kOutput, calls=%fused_computation.24 | convolution fusion | flops 907739136 | bytes 9043968 | tf_op jit(solution)/shard_map/sij,sjk->sik/dot_general | solution.py:55
  193.0 2.3 broadcast_in_dim.67
  195.3 2.6 scatter_fusion
  197.9 6.7 %all-to-all-start = ((bf16[16,768,128]{2,1,0:T(8,128)(2,1)}), bf16[16,768,128]{2,1,0:T(8,128)(2,1)S(1)}, u32[]{:S(2)}, u32[]{:S(2)}) async-start(bf16[16,768,128]{2,1,0:T(8,128)(2,1)} %scatter_fusion), calls=%async_computation | async-start | bytes 6291456 | tf_op jit(solution)/shard_map/all_to_all | solution.py:90
  205.2 47.3 %all-to-all-done = bf16[16,768,128]{2,1,0:T(8,128)(2,1)S(1)} async-done(((bf16[16,768,128]{2,1,0:T(8,128)(2,1)}), bf16[16,768,128]{2,1,0:T(8,128)(2,1)S(1)}, u32[]{:S(2)}, u32[]{:S(2)}) %all-to-all-start) | async-done | bytes 3145760 | tf_op jit(solution)/shard_map/all_to_all | solution.py:90
  252.4 1.7 gather_fusion.1
  254.2 8.3 %multiply_reduce_fusion.1 = f32[6,1536]{1,0:T(8,128)S(1)} fusion(bf16[6,768,1536]{2,1,0:T(8,128)(2,1)} %bitcast.73, bf16[6,768,128]{2,1,0:T(8,128)(2,1)} %gather_fusion.1, pred[6]{0:T(512)(128)(4,1)S(1)} %compare_and_fusion.1), kind=kOutput, calls=%fused_computation.11 | convolution fusion | flops 1816058880 | bytes 17731590 | tf_op jit(solution)/shard_map/tnm,tnx->tmx/dot_general | solution.py:93
  262.7 4.8 %collective-permute-start.1 = (f32[1,256]{1,0:T(1,128)S(1)}, f32[1,256]{1,0:T(1,128)S(1)}, u32[]{:S(2)}, u32[]{:S(2)}) collective-permute-start(f32[1,256]{1,0:T(1,128)S(1)} %bitcast.70), channel_id=1, source_target_pairs={{0,15},{1,0},{2,1},{3,2},{4,3},{5,4},{6,5},{7,6},{8,7},{9,8},{10,9... | collective-permute-start | bytes 3080 | tf_op jit(solution)/shard_map/ppermute | solution.py:17
  267.5 0.9 collective-permute-done
  268.5 10.1 %all_to_all.10 = f32[8,1,128]{2,1,0:T(1,128)S(1)} all-to-all(f32[8,1,128]{2,1,0:T(1,128)S(1)} %transpose_reshape_reshape.3), channel_id=1, replica_groups=mesh['row'=8,'grid'=16] {'row'}, dimensions={0} | all-to-all | bytes 8192 | tf_op jit(solution)/shard_map/all_to_all | solution.py:27
  278.6 0.5 reduce_sum.54
  (45 shorter events, 1.4 us)
Async XLA Ops:
  6.5 1.0 copy-start
  6.5 55.9 %all-gather.3.cloned.1.call-start = ((), (), s32[]{:S(2)}) async-start(), calls=%async_computation.2 | async-start | bytes 9437184 | tf_op jit(solution)/shard_map/all_gather | solution.py:66
  7.3 112.1 %all-gather.5.cloned.1.call-start = ((), (), s32[]{:S(2)}) async-start(), calls=%async_computation.3 | async-start | bytes 9437184 | tf_op jit(solution)/shard_map/all_gather | solution.py:69
  62.5 6.8 %copy-start.4 = (s32[1,1,3,6]{3,1,2,0:T(1,128)S(1)}, s32[1,1,3,6]{3,1,2,0:T(1,128)}, u32[]{:S(2)}) copy-start(s32[1,1,3,6]{3,1,2,0:T(1,128)} %param.14) | copy-start | bytes 220
  62.5 7.8 %copy-start.3 = (s32[1,16,3]{1,0,2:T(1,128)S(1)}, s32[1,16,3]{1,0,2:T(1,128)}, u32[]{:S(2)}) copy-start(s32[1,16,3]{1,0,2:T(1,128)} %param.15) | copy-start | bytes 580
  161.5 5.2 %copy-start.2 = (f32[6,128,6,128]{3,1,0,2:T(8,128)S(1)}, f32[6,128,6,128]{3,1,0,2:T(8,128)}, u32[]{:S(2)}) copy-start(f32[6,128,6,128]{3,1,0,2:T(8,128)} %compare_select_fusion) | copy-start | bytes 7077892
  187.7 7.7 %copy-start.5 = (s32[3]{0:T(128)S(1)}, s32[3]{0:T(128)}, u32[]{:S(2)}) copy-start(s32[3]{0:T(128)} %fusion.29) | copy-start | bytes 40
  197.9 54.5 %all-to-all-start = ((bf16[16,768,128]{2,1,0:T(8,128)(2,1)}), bf16[16,768,128]{2,1,0:T(8,128)(2,1)S(1)}, u32[]{:S(2)}, u32[]{:S(2)}) async-start(bf16[16,768,128]{2,1,0:T(8,128)(2,1)} %scatter_fusion), calls=%async_computation | async-start | bytes 6291456 | tf_op jit(solution)/shard_map/all_to_all | solution.py:90
  254.2 25.0 %copy-start.1 = (bf16[1,2,8,128,128]{4,3,2,1,0:T(8,128)(2,1)S(1)}, bf16[1,2,8,128,128]{4,3,2,1,0:T(8,128)(2,1)}, u32[]{:S(2)}) copy-start(bf16[1,2,8,128,128]{4,3,2,1,0:T(8,128)(2,1)} %param.12) | copy-start | bytes 1572868
  262.6 5.8 %collective-permute-start = (f32[1,256]{1,0:T(1,128)S(1)}, f32[1,256]{1,0:T(1,128)S(1)}, u32[]{:S(2)}, u32[]{:S(2)}) collective-permute-start(f32[1,256]{1,0:T(1,128)S(1)} %bitcast.71), channel_id=1, source_target_pairs={{0,1},{1,2},{2,3},{3,4},{4,5},{5,6},{6,7},{7,8},{8,9},{9,10},{10,1... | collective-permute-start | bytes 3080 | tf_op jit(solution)/shard_map/ppermute | solution.py:17
  262.7 5.8 %collective-permute-start.1 = (f32[1,256]{1,0:T(1,128)S(1)}, f32[1,256]{1,0:T(1,128)S(1)}, u32[]{:S(2)}, u32[]{:S(2)}) collective-permute-start(f32[1,256]{1,0:T(1,128)S(1)} %bitcast.70), channel_id=1, source_target_pairs={{0,15},{1,0},{2,1},{3,2},{4,3},{5,4},{6,5},{7,6},{8,7},{9,8},{10,9... | collective-permute-start | bytes 3080 | tf_op jit(solution)/shard_map/ppermute | solution.py:17
Sparse Core Ops, SparseCore 0:
  9.1 53.3 all-gather.2
  69.4 49.8 all-gather.4
where the time goes:
time: 287 us; the launch traced here: 286 us
  waiting for transfers between devices  145 us (51%)
  local copies, waits for them, and re-layouts  53.8 us (19%)
  matrix products  33.8 us (12%)
  other arithmetic  17.7 us (6%)
  between operations  14.2 us (5%)
  starting transfers between devices  11.5 us (4%)
  blocking collectives  10.1 us (4%)
    all_gather x1, waiting for transfers between devices, on_device(): lax.all_gather(h_rows, 'row', axis=1, tiled=True)[0]  53.6 us
    all_to_all x1, waiting for transfers between devices, on_device(): lax.all_to_all(outgoing, 'grid', split_axis=0, concat_axis=0, tiled=True)  47.3 us
    all_gather x1, waiting for transfers between devices, on_device(): lax.all_gather(product.astype(jnp.bfloat16), 'row', axis=0, tiled=True)  42.2 us
    gather x2, local copies, waits for them, and re-layouts, extract(): rows = jnp.take(blocks4, picks, axis=0)  18.9 us
    gather x4, local copies, waits for them, and re-layouts, extract(): return jnp.take(rows, picks, axis=2).reshape(ORDER, ORDER)  17.6 us
    dot_general x1, matrix products, sign_batch(): jnp.einsum('sij,sjk->sik', first, helper, preferred_element_type=jnp.floa...  12.1 us
    unnamed x15, local copies, waits for them, and re-layouts  10.2 us
    all_to_all x1, blocking collectives, sum_at_owner(): lax.all_to_all(parts, axis, split_axis=0, concat_axis=0, tiled=True)  10.1 us
  transfers between devices with their start and end apart: 5, of which 4 were waited for; matrix products, arithmetic and copies ran while one was open for 3% of the time, Pallas kernels for 0%

commit v1 on v0

v1 whole, which is shorter than its diff:
```python
import jax
import jax.numpy as jnp
from jax import lax
from jax.experimental import pallas as pl
from jax.experimental.pallas import tpu as pltpu
from jax.sharding import PartitionSpec as P

BLK = 128
SUB_BLK = 6
NZ = 8
SUB_DEV = 3
OWN_MAX = 6
PLANE = 256
DEPTH = 4
MARG = 1
ORDER = 768
KB = 16
NREG = 2048
HALF = 8

X_DN, X_UP, X_SIB, X_FAR_A, X_FAR_B, X_SDN, X_SUP, X_SFAR_A, X_SFAR_B = range(9)
T_DN, T_UP, T_SIB, T_FAR, T_SDN, T_SUP, T_SFAR = range(9, 16)
H_DN, H_UP, H_SIB, H_FAR, H_SDN, H_SUP, H_SFAR = range(16, 30, 2)
N_SEM = 30


def eye_like(rows, cols, first_row):
    row = lax.broadcasted_iota(jnp.int32, (rows, cols), 0) + first_row
    col = lax.broadcasted_iota(jnp.int32, (rows, cols), 1)
    return row == col


def region_kernel(
    h_in, x_in, inv_in, same_in, picks, mu_in, out,
    h_own, h_dn, h_up, h_far, x_all, table, table_s, lhs, rhs, total, z0, y0, z1, y1,
    send_sem, recv_sem, own_sem, table_sem,
):
    r = lax.axis_index("row")
    g = lax.axis_index("grid")
    y = r // 2
    core = r - 2 * y
    sib = 2 * y + 1 - core
    y_up, y_dn, y_far = lax.rem(y + 1, 4), lax.rem(y + 3, 4), lax.rem(y + 2, 4)
    up, dn = 2 * y_up + core, 2 * y_dn + core

    barrier = pltpu.get_barrier_semaphore()
    for other in (up, dn, sib):
        pl.semaphore_signal(
            barrier, inc=1, device_id=(other, g), device_id_type=pl.DeviceIdType.MESH
        )

    for b in range(KB):
        pltpu.make_async_copy(
            h_in.at[:, b * BLK : (b + 1) * BLK], h_own.at[core, b], own_sem
        ).start()
    for i in range(2):
        for z in range(NZ):
            block = x_in[i, z].astype(jnp.float32)
            for w in range(z + 1, NZ):
                block += x_in[i, w].astype(jnp.float32) * same_in[(i * NZ + z) * NZ + w]
            x_all[2 * r + i, z] = block.astype(jnp.bfloat16)
    for i in range(KB):
        x_all[i, NZ] = jnp.zeros((BLK, BLK), jnp.bfloat16)
    table[pl.ds(2 * r, 2)] = inv_in[...]
    pl.semaphore_wait(barrier, 3)

    copies = {}

    def send(slot, src, dst, device):
        copy = pltpu.make_async_remote_copy(
            src_ref=src, dst_ref=dst, send_sem=send_sem.at[slot], recv_sem=recv_sem.at[slot],
            device_id=(device, g), device_id_type=pl.DeviceIdType.MESH,
        )
        copy.start()
        copies[slot] = copy

    def x_rows(origin):
        return x_all.at[pl.ds(2 * origin, 2), pl.ds(0, NZ)]

    def x_row(origin, i):
        return x_all.at[2 * origin + i, pl.ds(0, NZ)]

    for slot, device in ((X_DN, up), (X_UP, dn), (X_SIB, sib)):
        send(slot, x_rows(r), x_rows(r), device)
    def t_rows(origin):
        return table.at[pl.ds(2 * origin, 2)]

    for slot, device in ((T_DN, up), (T_UP, dn), (T_SIB, sib)):
        send(slot, t_rows(r), t_rows(r), device)

    def half(ref, which):
        return ref.at[core, pl.ds(which * HALF, HALF)]

    def h_half(which):
        return half(h_own, which)

    pltpu.make_async_copy(h_own.at[core], h_own.at[core], own_sem).wait()
    send(H_DN, h_half(0), half(h_dn, 0), up)
    send(H_UP + 1, h_half(1), half(h_up, 1), dn)
    send(H_SIB, h_half(0), half(h_own, 0), sib)
    send(H_SIB + 1, h_half(1), half(h_own, 1), sib)
    send(H_DN + 1, h_half(1), half(h_dn, 1), up)
    send(H_UP, h_half(0), half(h_up, 0), dn)

    copies[X_DN].wait_recv()
    send(X_FAR_A, x_row(dn, 0), x_row(dn, 0), up)
    send(X_SDN, x_rows(dn), x_rows(dn), sib)
    copies[X_UP].wait_recv()
    send(X_FAR_B, x_row(up, 1), x_row(up, 1), dn)
    send(X_SUP, x_rows(up), x_rows(up), sib)
    far = 2 * y_far + core
    copies[T_DN].wait_recv()
    send(T_FAR, t_rows(dn), t_rows(dn), up)
    send(T_SDN, t_rows(dn), t_rows(dn), sib)
    copies[T_UP].wait_recv()
    send(T_SUP, t_rows(up), t_rows(up), sib)
    copies[X_FAR_A].wait_recv()
    send(X_SFAR_A, x_row(far, 0), x_row(far, 0), sib)
    copies[X_FAR_B].wait_recv()
    send(X_SFAR_B, x_row(far, 1), x_row(far, 1), sib)
    copies[T_FAR].wait_recv()
    send(T_SFAR, t_rows(far), t_rows(far), sib)

    copies[H_DN].wait_recv()
    send(H_FAR, half(h_dn, 0), half(h_far, 0), up)
    send(H_SDN, half(h_dn, 0), half(h_dn, 0), sib)
    copies[H_UP + 1].wait_recv()
    send(H_FAR + 1, half(h_up, 1), half(h_far, 1), dn)
    send(H_SUP + 1, half(h_up, 1), half(h_up, 1), sib)

    for slot in (X_SIB, X_SDN, X_SUP, X_SFAR_A, X_SFAR_B, T_SIB, T_SDN, T_SUP, T_SFAR):
        copies[slot].wait_recv()
    table_copy = pltpu.make_async_copy(table, table_s, table_sem)
    table_copy.start()
    table_copy.wait()

    def accumulate(h_ref, chip, first):
        def one(k, carry):
            for b in range(SUB_BLK):
                pick = picks[k * SUB_BLK + b]
                for j in range(4):
                    z = table_s[pick, 0, 4 * chip + j]
                    lhs[b * BLK : (b + 1) * BLK, j * BLK : (j + 1) * BLK] = x_all[pick, z]
                for c in range(2):
                    rhs[c * 2 * BLK : (c + 1) * 2 * BLK, b * BLK : (b + 1) * BLK] = h_ref[
                        c, pick
                    ]
            part = jnp.dot(lhs[...], rhs[...], preferred_element_type=jnp.float32)
            if first:
                total[k] = part
            else:
                total[k] += part
            return carry

        lax.fori_loop(0, SUB_DEV, one, 0)

    copies[H_SIB].wait_recv()
    copies[H_SIB + 1].wait_recv()
    accumulate(h_own, y, True)

    copies[H_DN + 1].wait_recv()
    send(H_SDN + 1, half(h_dn, 1), half(h_dn, 1), sib)
    copies[H_UP].wait_recv()
    send(H_SUP, half(h_up, 0), half(h_up, 0), sib)
    copies[H_SDN].wait_recv()
    copies[H_SDN + 1].wait_recv()
    accumulate(h_dn, y_dn, False)
    copies[H_SUP].wait_recv()
    copies[H_SUP + 1].wait_recv()
    accumulate(h_up, y_up, False)

    copies[H_FAR].wait_recv()
    send(H_SFAR, half(h_far, 0), half(h_far, 0), sib)
    copies[H_FAR + 1].wait_recv()
    send(H_SFAR + 1, half(h_far, 1), half(h_far, 1), sib)
    copies[H_SFAR].wait_recv()
    copies[H_SFAR + 1].wait_recv()
    accumulate(h_far, y_far, False)

    mu = mu_in[0]

    def sign(k, carry):
        mat = total[k].astype(jnp.bfloat16).astype(jnp.float32)
        shifted = mat - jnp.where(eye_like(ORDER, ORDER, 0), mu, 0.0)
        scale = jnp.sqrt(jnp.sum(shifted * shifted, axis=(0, 1), keepdims=True) / ORDER + 1e-06)
        z0[...] = (shifted * (0.5 / scale)).astype(jnp.bfloat16)
        for m in range(3):
            rows = pl.ds(m * 2 * BLK, 2 * BLK)
            square = jnp.dot(z0[rows, :], z0[...], preferred_element_type=jnp.float32)
            diag = jnp.where(eye_like(2 * BLK, ORDER, m * 2 * BLK), 3.0, 0.0)
            y0[rows, :] = (diag - square).astype(jnp.bfloat16)
        for m in range(3):
            rows = pl.ds(m * 2 * BLK, 2 * BLK)
            step = jnp.dot(z0[rows, :], y0[...], preferred_element_type=jnp.float32)
            z1[rows, :] = (0.5 * step).astype(jnp.bfloat16)
        square = jnp.dot(z1[...], z1[:, :BLK], preferred_element_type=jnp.float32)
        eye = eye_like(ORDER, BLK, 0)
        y1[...] = (jnp.where(eye, 3.0, 0.0) - square).astype(jnp.bfloat16)
        last = 0.5 * jnp.dot(z1[...], y1[...], preferred_element_type=jnp.float32)
        out[k] = (0.5 * (jnp.where(eye, 1.0, 0.0) - last)).astype(jnp.bfloat16)
        return carry

    lax.fori_loop(0, SUB_DEV, sign, 0)
    for copy in copies.values():
        copy.wait_send()


def region(h_rows, x_blocks, inverse, same, picks, mu):
    vmem = pl.BlockSpec(memory_space=pltpu.VMEM)
    smem = pl.BlockSpec(memory_space=pltpu.SMEM)
    h_buf = pltpu.VMEM((2, KB, 2 * BLK, BLK), jnp.bfloat16)
    square = pltpu.VMEM((ORDER, ORDER), jnp.bfloat16)
    return pl.pallas_call(
        region_kernel,
        out_shape=jax.ShapeDtypeStruct((SUB_DEV, ORDER, BLK), jnp.bfloat16),
        in_specs=[pl.BlockSpec(memory_space=pl.ANY), vmem, vmem, smem, smem, smem],
        out_specs=vmem,
        scratch_shapes=[
            h_buf, h_buf, h_buf, h_buf,
            pltpu.VMEM((KB, NZ + 1, BLK, BLK), jnp.bfloat16),
            pltpu.VMEM((KB, 8, BLK), jnp.int32),
            pltpu.SMEM((KB, 8, BLK), jnp.int32),
            pltpu.VMEM((ORDER, 4 * BLK), jnp.bfloat16),
            pltpu.VMEM((4 * BLK, ORDER), jnp.bfloat16),
            pltpu.VMEM((SUB_DEV, ORDER, ORDER), jnp.float32),
            square, square, square,
            pltpu.VMEM((ORDER, BLK), jnp.bfloat16),
            pltpu.SemaphoreType.DMA((N_SEM,)),
            pltpu.SemaphoreType.DMA((N_SEM,)),
            pltpu.SemaphoreType.DMA,
            pltpu.SemaphoreType.DMA,
        ],
        compiler_params=pltpu.CompilerParams(
            collective_id=0, has_side_effects=True, vmem_limit_bytes=56 << 20
        ),
        name="region",
    )(h_rows, x_blocks, inverse, same, picks, mu)


def from_behind(value, axis, steps):
    count = lax.axis_size(axis)
    pairs = [(source, (source + steps) % count) for source in range(count)]
    return lax.ppermute(value, axis, pairs)


def cut_along(value, dim, devices):
    before, after = (value.shape[:dim], value.shape[dim + 1 :])
    return jnp.moveaxis(value.reshape(*before, devices, -1, *after), dim, 0)


def sum_at_owner(value, axis, dim):
    parts = cut_along(value, dim, lax.axis_size(axis))
    arrived = lax.all_to_all(parts, axis, split_axis=0, concat_axis=0, tiled=True)
    return arrived.sum(axis=0)


def inverse_table(cols):
    found = cols[:, :, None] == jnp.arange(KB, dtype=jnp.int32)[None, None, :]
    first = jnp.min(jnp.where(found, jnp.arange(NZ, dtype=jnp.int32)[None, :, None], NZ), axis=1)
    return jnp.zeros((2, 8, BLK), jnp.int32).at[:, :, :KB].set(first[:, None, :])


def same_column(cols):
    return (cols[:, :, None] == cols[:, None, :]).astype(jnp.float32).reshape(-1)


def on_device(h_rows, x_blocks, x_cols, sub_blocks, owners, shift_mu, orbitals):
    built = region(
        h_rows[0], x_blocks[0], inverse_table(x_cols[0]), same_column(x_cols[0]),
        sub_blocks.reshape(-1), shift_mu,
    )
    ngrid = lax.axis_size("grid")
    myself = lax.axis_index("grid")
    table = owners[0]
    targets = lax.dynamic_index_in_dim(table, myself, 0, keepdims=False)
    hit = table == myself
    has = jnp.any(hit, axis=1)
    place = jnp.cumsum(has.astype(jnp.int32)) - 1
    select = has[None, :] & (place[None, :] == jnp.arange(OWN_MAX, dtype=jnp.int32)[:, None])
    selint = select.astype(jnp.int32)
    source = jnp.sum(selint * jnp.arange(ngrid, dtype=jnp.int32)[None, :], axis=1)
    live = jnp.any(select, axis=1)
    outgoing = jnp.zeros((ngrid, ORDER, BLK), jnp.bfloat16).at[targets].set(built)
    incoming = lax.all_to_all(outgoing, "grid", split_axis=0, concat_axis=0, tiled=True)
    columns = jnp.take(incoming, source, axis=0)
    phi = orbitals[0, 0]
    proj = jnp.einsum("tnm,tnx->tmx", columns, phi, preferred_element_type=jnp.float32)
    values = jnp.sum(proj * phi[:, :BLK, :].astype(jnp.float32), axis=1)
    window = jnp.sum(jnp.where(live[:, None], values, 0.0), axis=0).reshape(DEPTH + 2 * MARG, PLANE)
    core = window[MARG : MARG + DEPTH]
    from_prev = from_behind(window[MARG + DEPTH :], "grid", 1)
    from_next = from_behind(window[:MARG], "grid", -1)
    core = core.at[:MARG].add(from_prev)
    core = core.at[DEPTH - MARG :].add(from_next)
    return sum_at_owner(core.reshape(1, DEPTH * PLANE), "row", 1)


def solution(mesh):
    in_specs = (
        P("grid", "row", None),
        P("grid", "row", None, None, None),
        P("grid", "row", None),
        P("row", "grid", None, None),
        P("row", None, None),
        P(),
        P("row", "grid", None, None, None),
    )
    out_specs = P("grid", "row")
    return jax.shard_map(
        on_device, mesh=mesh, in_specs=in_specs, out_specs=out_specs, check_vma=False
    )
```

time: 287 us -> 171 us (0.60)
  waiting for transfers between devices: 145 us -> 49.7 us
  Pallas kernels: 0 us -> 78.2 us
  local copies, waits for them, and re-layouts: 53.8 us -> 9.54 us
  matrix products: 33.8 us -> 8.29 us
  other arithmetic: 17.7 us -> 3.37 us
  between operations: 14.2 us -> 0.75 us
    all_gather x2 -> x0, waiting for transfers between devices: 95.9 us -> none  [the longest x1 53.6 us: on_device(): lax.all_gather(h_rows, 'row', axis=1, tiled=True)[0]]
    pallas_call x0 -> x1, Pallas kernels: none -> 78.2 us  [region(): pl.pallas_call(region_kernel, out_shape=jax.ShapeDtypeStruct((SUB_DEV, OR...]
    gather x6 -> x0, local copies, waits for them, and re-layouts: 36.5 us -> none  [the longest x2 18.9 us: extract(): rows = jnp.take(blocks4, picks, axis=0)]
    dot_general x4 -> x0, matrix products: 25.5 us -> none  [the longest x1 12.1 us: sign_batch(): jnp.einsum('sij,sjk->sik', first, helper, preferred_element_type=jnp.floa...]
    unnamed x15 -> x4, local copies, waits for them, and re-layouts: 10.2 us -> 0.01 us
    select_n x1 -> x0, other arithmetic: 8.27 us -> none  [extract(): rows = jnp.take(blocks4, picks, axis=0)]
    mul x4 -> x0, other arithmetic: 5.13 us -> none  [the longest x1 2.46 us: sign_batch(): helper = (3.0 * eye[None] - square).astype(jnp.bfloat16)]
  transfers between devices with their start and end apart: 5 -> 3, of which waited for: 4 -> 2; matrix products, arithmetic and copies ran while one was open for 3% -> 0% of each run, Pallas kernels for 0% -> 0%
where the time goes in v1:
time: 171 us
  Pallas kernels  78.2 us (46%)
  waiting for transfers between devices  49.7 us (29%)
  starting transfers between devices  12.6 us (7%)
  local copies, waits for them, and re-layouts  9.54 us (6%)
  blocking collectives  8.59 us (5%)
  matrix products  8.29 us (5%)
  other arithmetic  3.37 us (2%)
    pallas_call x1, Pallas kernels, region(): pl.pallas_call(region_kernel, out_shape=jax.ShapeDtypeStruct((SUB_DEV, OR...  78.2 us
    all_to_all x1, waiting for transfers between devices, on_device(): lax.all_to_all(outgoing, 'grid', split_axis=0, concat_axis=0, tiled=True)  48.8 us
    all_to_all x1, blocking collectives, sum_at_owner(): lax.all_to_all(parts, axis, split_axis=0, concat_axis=0, tiled=True)  8.59 us
    dot_general x1, matrix products, on_device(): jnp.einsum('tnm,tnx->tmx', columns, phi, preferred_element_type=jnp.float32)  8.29 us
    all_to_all x1, starting transfers between devices, on_device(): lax.all_to_all(outgoing, 'grid', split_axis=0, concat_axis=0, tiled=True)  7.72 us
    ppermute x2, starting transfers between devices, from_behind(): return lax.ppermute(value, axis, pairs)  4.85 us
  transfers between devices with their start and end apart: 3, of which 2 were waited for; matrix products, arithmetic and copies ran while one was open for 0% of the time, Pallas kernels for 0%

profile of v1, /device:TPU:1, one launch (start us, length us, event | category | flops | bytes accessed | tf_op | source)
XLA Modules:
  0.0 171.1 jit_solution(15737036202251706744)
XLA Ops:
  0.0 0.8 select_reduce_fusion.1
  0.8 0.8 compare_convert_fusion
  1.6 0.9 dynamic-slice_reduce_fusion
  2.5 0.6 scatter.12.inv_in
  3.1 0.6 reshape.192.same_in
  3.7 0.7 reduce.10
  4.4 0.6 reshape.189.picks
  5.7 78.2 %region.1 = bf16[3,768,128]{2,1,0:T(8,128)(2,1)} custom-call(bf16[256,2048]{1,0:T(8,128)(2,1)} %bitcast.19, bf16[2,8,128,128]{3,2,1,0:T(8,128)(2,1)} %bitcast.20, s32[2,8,128]{2,1,0:T(8,128)} %scatter.12.inv_in, f32[128]{0:T(128)} %reshape.192.same_in, s32[18]{0:T(128)} %reshape.189.picks, f32[1]{0:T(128)S(6)} %copy.19.mu_in), custom_call_target="tpu_custom_call" | custom-call | tf_op jit(solution)/shard_map/region/pallas_call | solution.py:213
  83.9 0.0 copy-start
  83.9 2.3 %broadcast_in_dim.52 = bf16[16,768,128]{2,1,0:T(8,128)(2,1)} broadcast(bf16[]{:T(256)} %constant.119.clone.1), dimensions={} | broadcast | bytes 3145730 | tf_op jit(solution)/shard_map/broadcast_in_dim | solution.py:283
  86.2 0.0 copy-done
  86.2 2.6 %scatter_fusion = bf16[16,768,128]{2,1,0:T(8,128)(2,1)} fusion(bf16[16,768,128]{2,1,0:T(8,128)(2,1)} %broadcast_in_dim.52, s32[3]{0:T(128)S(1)} %fusion.5, bf16[3,768,128]{2,1,0:T(8,128)(2,1)S(1)} %copy-done), kind=kCustom, calls=%fused_computation.1 | custom fusion | bytes 1769484 | tf_op jit(solution)/shard_map/scatter | solution.py:283
  88.8 0.0 copy-start.1
  88.8 7.7 %all-to-all-start = ((bf16[16,768,128]{2,1,0:T(8,128)(2,1)}), bf16[16,768,128]{2,1,0:T(8,128)(2,1)S(1)}, u32[]{:S(2)}, u32[]{:S(2)}) async-start(bf16[16,768,128]{2,1,0:T(8,128)(2,1)} %scatter_fusion), calls=%async_computation | async-start | bytes 6291456 | tf_op jit(solution)/shard_map/all_to_all | solution.py:284
  96.5 0.0 copy-done.1
  96.6 0.1 copy.13
  96.7 0.1 add_reduce_fusion
  96.8 0.1 select_reduce_fusion.2
  96.9 0.1 fusion.4
  97.1 48.8 %all-to-all-done = bf16[16,768,128]{2,1,0:T(8,128)(2,1)S(1)} async-done(((bf16[16,768,128]{2,1,0:T(8,128)(2,1)}), bf16[16,768,128]{2,1,0:T(8,128)(2,1)S(1)}, u32[]{:S(2)}, u32[]{:S(2)}) %all-to-all-start) | async-done | bytes 3145760 | tf_op jit(solution)/shard_map/all_to_all | solution.py:284
  145.9 1.7 %gather_fusion = bf16[6,768,128]{2,1,0:T(8,128)(2,1)} fusion(bf16[16,768,128]{2,1,0:T(8,128)(2,1)S(1)} %all-to-all-done, s32[1024]{0:T(1024)S(1)} %pad_clamp_fusion), kind=kCustom, calls=%fused_computation | custom fusion | bytes 2359320 | tf_op jit(solution)/shard_map/jit(_take)/gather | solution.py:285
  147.6 8.3 %multiply_reduce_fusion = f32[6,1536]{1,0:T(8,128)S(1)} fusion(bf16[6,768,1536]{2,1,0:T(8,128)(2,1)} %bitcast.26, bf16[6,768,128]{2,1,0:T(8,128)(2,1)} %gather_fusion, pred[6]{0:T(512)(128)(4,1)S(1)} %compare_and_fusion), kind=kOutput, calls=%fused_computation.2 | convolution fusion | flops 1816058880 | bytes 17731590 | tf_op jit(solution)/shard_map/tnm,tnx->tmx/dot_general | solution.py:287
  155.9 0.1 select_reduce_fusion
  156.0 0.1 collective-permute-start
  156.1 4.8 %collective-permute-start.1 = (f32[1,256]{1,0:T(1,128)S(1)}, f32[1,256]{1,0:T(1,128)S(1)}, u32[]{:S(2)}, u32[]{:S(2)}) collective-permute-start(f32[1,256]{1,0:T(1,128)S(1)} %bitcast.24), channel_id=1, source_target_pairs={{0,15},{1,0},{2,1},{3,2},{4,3},{5,4},{6,5},{7,6},{8,7},{9,8},{10,9... | collective-permute-start | bytes 3080 | tf_op jit(solution)/shard_map/ppermute | solution.py:243
  160.9 0.9 collective-permute-done
  161.9 0.0 collective-permute-done.1
  161.9 8.6 %all_to_all.10 = f32[8,1,128]{2,1,0:T(1,128)S(1)} all-to-all(f32[8,1,128]{2,1,0:T(1,128)S(1)} %transpose_reshape_reshape.3), channel_id=1, replica_groups=mesh['row'=8,'grid'=16] {'row'}, dimensions={0} | all-to-all | bytes 8192 | tf_op jit(solution)/shard_map/all_to_all | solution.py:253
  170.5 0.5 reduce_sum.44
  (16 shorter events, 0.2 us)
Async XLA Ops:
  83.9 2.3 %copy-start = (bf16[3,768,128]{2,1,0:T(8,128)(2,1)S(1)}, bf16[3,768,128]{2,1,0:T(8,128)(2,1)}, u32[]{:S(2)}) copy-start(bf16[3,768,128]{2,1,0:T(8,128)(2,1)} %region.1) | copy-start | bytes 1769476
  88.8 7.7 %copy-start.1 = (s32[1,16,3]{1,0,2:T(1,128)S(1)}, s32[1,16,3]{1,0,2:T(1,128)}, u32[]{:S(2)}) copy-start(s32[1,16,3]{1,0,2:T(1,128)} %param.17) | copy-start | bytes 580
  88.8 57.1 %all-to-all-start = ((bf16[16,768,128]{2,1,0:T(8,128)(2,1)}), bf16[16,768,128]{2,1,0:T(8,128)(2,1)S(1)}, u32[]{:S(2)}, u32[]{:S(2)}) async-start(bf16[16,768,128]{2,1,0:T(8,128)(2,1)} %scatter_fusion), calls=%async_computation | async-start | bytes 6291456 | tf_op jit(solution)/shard_map/all_to_all | solution.py:284
  156.0 5.8 %collective-permute-start = (f32[1,256]{1,0:T(1,128)S(1)}, f32[1,256]{1,0:T(1,128)S(1)}, u32[]{:S(2)}, u32[]{:S(2)}) collective-permute-start(f32[1,256]{1,0:T(1,128)S(1)} %bitcast.25), channel_id=1, source_target_pairs={{0,1},{1,2},{2,3},{3,4},{4,5},{5,6},{6,7},{7,8},{8,9},{9,10},{10,1... | collective-permute-start | bytes 3080 | tf_op jit(solution)/shard_map/ppermute | solution.py:243
  156.1 5.8 %collective-permute-start.1 = (f32[1,256]{1,0:T(1,128)S(1)}, f32[1,256]{1,0:T(1,128)S(1)}, u32[]{:S(2)}, u32[]{:S(2)}) collective-permute-start(f32[1,256]{1,0:T(1,128)S(1)} %bitcast.24), channel_id=1, source_target_pairs={{0,15},{1,0},{2,1},{3,2},{4,3},{5,4},{6,5},{7,6},{8,7},{9,8},{10,9... | collective-permute-start | bytes 3080 | tf_op jit(solution)/shard_map/ppermute | solution.py:243

commit v2 on v1

--- a/solution.py
+++ b/solution.py
@@ -17,6 +17,8 @@
 KB = 16
 NREG = 2048
 HALF = 8
+SPLIT = 384
+EXT = 1536
 
 X_DN, X_UP, X_SIB, X_FAR_A, X_FAR_B, X_SDN, X_SUP, X_SFAR_A, X_SFAR_B = range(9)
 T_DN, T_UP, T_SIB, T_FAR, T_SDN, T_SUP, T_SFAR = range(9, 16)
@@ -31,24 +33,54 @@
 
 
 def region_kernel(
-    h_in, x_in, inv_in, same_in, picks, mu_in, out,
+    h_in, x_in, inv_in, same_in, picks, mu_in, which_in, slots_in, live_in, phi_in, out,
     h_own, h_dn, h_up, h_far, x_all, table, table_s, lhs, rhs, total, z0, y0, z1, y1,
-    send_sem, recv_sem, own_sem, table_sem,
+    phi, line_x, line_z, pack_x, pack_z, pass_x, pass_z, got_x, got_z, pieces, sums,
+    send_sem, recv_sem, own_sem, table_sem, phi_sem,
+    line_send, line_recv, swap_send, swap_recv, sum_send, sum_recv,
 ):
     r = lax.axis_index("row")
     g = lax.axis_index("grid")
+    gz = g // 4
+    gx = g - 4 * gz
     y = r // 2
     core = r - 2 * y
     sib = 2 * y + 1 - core
     y_up, y_dn, y_far = lax.rem(y + 1, 4), lax.rem(y + 3, 4), lax.rem(y + 2, 4)
     up, dn = 2 * y_up + core, 2 * y_dn + core
 
+    x_next = 4 * gz + lax.rem(gx + 1, 4)
+    x_prev = 4 * gz + lax.rem(gx + 3, 4)
+    z_next = 4 * lax.rem(gz + 1, 4) + gx
+    z_prev = 4 * lax.rem(gz + 3, 4) + gx
+    brick_next = lax.rem(g + 1, 16)
+    brick_prev = lax.rem(g + 15, 16)
+
+    sums[...] = jnp.zeros_like(sums)
     barrier = pltpu.get_barrier_semaphore()
-    for other in (up, dn, sib):
+
+    def greet(row, grid):
         pl.semaphore_signal(
-            barrier, inc=1, device_id=(other, g), device_id_type=pl.DeviceIdType.MESH
-        )
-
+            barrier, inc=1, device_id=(row, grid), device_id_type=pl.DeviceIdType.MESH
+        )
+
+    for step in range(1, 8):
+        greet(lax.rem(r + step, 8), g)
+    for other in (x_next, x_prev, z_next, z_prev):
+        greet(r, other)
+
+    @pl.when(r < 2)
+    def _():
+        for row in range(8):
+            greet(row, brick_prev)
+
+    @pl.when(r >= 6)
+    def _():
+        for row in range(8):
+            greet(row, brick_next)
+
+    phi_copy = pltpu.make_async_copy(phi_in, phi, phi_sem)
+    phi_copy.start()
     for b in range(KB):
         pltpu.make_async_copy(
             h_in.at[:, b * BLK : (b + 1) * BLK], h_own.at[core, b], own_sem
@@ -62,7 +94,7 @@
     for i in range(KB):
         x_all[i, NZ] = jnp.zeros((BLK, BLK), jnp.bfloat16)
     table[pl.ds(2 * r, 2)] = inv_in[...]
-    pl.semaphore_wait(barrier, 3)
+    pl.semaphore_wait(barrier, 15)
 
     copies = {}
 
@@ -179,6 +211,28 @@
 
     mu = mu_in[0]
 
+    def line_copy(way, k):
+        line, me, before, after = (
+            (line_x, gx, x_prev, x_next) if way < 4 else (line_z, gz, z_prev, z_next)
+        )
+        kind = way % 4
+        source = lax.rem(me + (0, 0, 3, 1)[kind], 4)
+        rows = (pl.ds(0, SPLIT), pl.ds(0, SPLIT), pl.ds(0, SPLIT // 2), pl.ds(SPLIT // 2, SPLIT // 2))
+        part = line.at[source, k, rows[kind]]
+        return pltpu.make_async_remote_copy(
+            src_ref=part, dst_ref=part,
+            send_sem=line_send.at[way, k], recv_sem=line_recv.at[way, k],
+            device_id=(r, (after, before, after, before)[kind]),
+            device_id_type=pl.DeviceIdType.MESH,
+        )
+
+    def pass_on(k):
+        for first in (0, 4):
+            line_copy(first, k).wait_recv()
+            line_copy(first + 2, k).start()
+            line_copy(first + 1, k).wait_recv()
+            line_copy(first + 3, k).start()
+
     def sign(k, carry):
         mat = total[k].astype(jnp.bfloat16).astype(jnp.float32)
         shifted = mat - jnp.where(eye_like(ORDER, ORDER, 0), mu, 0.0)
@@ -197,23 +251,133 @@
         eye = eye_like(ORDER, BLK, 0)
         y1[...] = (jnp.where(eye, 3.0, 0.0) - square).astype(jnp.bfloat16)
         last = 0.5 * jnp.dot(z1[...], y1[...], preferred_element_type=jnp.float32)
-        out[k] = (0.5 * (jnp.where(eye, 1.0, 0.0) - last)).astype(jnp.bfloat16)
+        columns = (0.5 * (jnp.where(eye, 1.0, 0.0) - last)).astype(jnp.bfloat16)
+        line_x[gx, k] = columns[:SPLIT]
+        line_z[gz, k] = columns[SPLIT:]
+        for way in (0, 1, 4, 5):
+            line_copy(way, k).start()
+
+        @pl.when(k > 0)
+        def _():
+            pass_on(k - 1)
+
         return carry
 
     lax.fori_loop(0, SUB_DEV, sign, 0)
-    for copy in copies.values():
+    pass_on(SUB_DEV - 1)
+    for k in range(SUB_DEV):
+        for way in (2, 3, 6, 7):
+            line_copy(way, k).wait_recv()
+
+    for s in range(4):
+        for step in (2, 1, 3):
+            to_z = lax.rem(gz + step, 4)
+            pack_x[step, s] = line_x[s, which_in[(4 * gz + s) * 16 + 4 * to_z + gx]]
+            to_x = lax.rem(gx + step, 4)
+            pack_z[step, s] = line_z[s, which_in[(4 * s + gx) * 16 + 4 * gz + to_x]]
+
+    def swap(slot, src, dst, device):
+        return pltpu.make_async_remote_copy(
+            src_ref=src, dst_ref=dst,
+            send_sem=swap_send.at[slot], recv_sem=swap_recv.at[slot],
+            device_id=(r, device), device_id_type=pl.DeviceIdType.MESH,
+        )
+
+    def swaps(base, pack, passed, got, me, before, after):
+        first, last = pl.ds(0, 2), pl.ds(2, 2)
+        away = [
+            swap(base, pack.at[2, first], passed.at[0], after),
+            swap(base + 1, pack.at[2, last], passed.at[1], before),
+            swap(base + 2, pack.at[1], got.at[me], after),
+            swap(base + 3, pack.at[3], got.at[me], before),
+        ]
+        far = [
+            swap(base + 4, passed.at[0], got.at[lax.rem(me + 3, 4), first], after),
+            swap(base + 5, passed.at[1], got.at[lax.rem(me + 1, 4), last], before),
+        ]
+        return away, far
+
+    away_x, far_x = swaps(0, pack_x, pass_x, got_x, gz, z_prev, z_next)
+    away_z, far_z = swaps(6, pack_z, pass_z, got_z, gx, x_prev, x_next)
+    for one in (*away_x, *away_z):
+        one.start()
+    for s in range(4):
+        got_x[gz, s] = line_x[s, which_in[(4 * gz + s) * 16 + g]]
+        got_z[gx, s] = line_z[s, which_in[(4 * s + gx) * 16 + g]]
+    for i in range(2):
+        for away, far in ((away_x, far_x), (away_z, far_z)):
+            away[i].wait_recv()
+            far[i].start()
+    for one in (*away_x[2:], *away_z[2:], *far_x, *far_z):
+        one.wait_recv()
+    phi_copy.wait()
+
+    across = (((0,), (0,)), ((), ()))
+
+    def collocate(t, window):
+        from_z, from_x = slots_in[2 * t], slots_in[2 * t + 1]
+        top, low = got_x[from_z, from_x], got_z[from_x, from_z]
+        proj = lax.dot_general(
+            top, phi[t, :SPLIT], across, preferred_element_type=jnp.float32
+        ) + lax.dot_general(low, phi[t, SPLIT:], across, preferred_element_type=jnp.float32)
+        values = jnp.sum(proj * phi[t, :BLK].astype(jnp.float32), axis=0, keepdims=True)
+        return window + values * live_in[t]
+
+    window = lax.fori_loop(0, OWN_MAX, collocate, jnp.zeros((1, EXT), jnp.float32))
+    for i in range(EXT // BLK):
+        pieces[i] = window[:, i * BLK : (i + 1) * BLK]
+
+    def give(slot, piece, place, row, grid):
+        copy = pltpu.make_async_remote_copy(
+            src_ref=pieces.at[piece], dst_ref=sums.at[place],
+            send_sem=sum_send.at[slot], recv_sem=sum_recv.at[place],
+            device_id=(row, grid), device_id_type=pl.DeviceIdType.MESH,
+        )
+        copy.start()
+        return copy
+
+    given = []
+    for row in range(2):
+        given.append(give(7 + row, 10 + row, 8 + r, row, brick_next))
+        given.append(give(9 + row, row, 8 + r, 6 + row, brick_prev))
+    for step in range(1, 8):
+        row = lax.rem(r + step, 8)
+        given.append(give(step - 1, 2 + row, r, row, g))
+    sums[r] = pieces[2 + r]
+
+    def arrived(place):
+        pltpu.make_async_copy(sums.at[place], sums.at[place], sum_recv.at[place]).wait()
+
+    for step in range(1, 8):
+        arrived(lax.rem(r + step, 8))
+
+    @pl.when((r < 2) | (r >= 6))
+    def _():
+        for row in range(8):
+            arrived(8 + row)
+
+    out[...] = jnp.sum(sums[...], axis=0)
+    for copy in (*copies.values(), *away_x, *away_z, *far_x, *far_z, *given):
         copy.wait_send()
-
-
-def region(h_rows, x_blocks, inverse, same, picks, mu):
+    for k in range(SUB_DEV):
+        for way in range(8):
+            line_copy(way, k).wait_send()
+
+
+def region(h_rows, x_blocks, inverse, same, picks, mu, which, slots, live, orbitals):
     vmem = pl.BlockSpec(memory_space=pltpu.VMEM)
     smem = pl.BlockSpec(memory_space=pltpu.SMEM)
+    hbm = pl.BlockSpec(memory_space=pl.ANY)
     h_buf = pltpu.VMEM((2, KB, 2 * BLK, BLK), jnp.bfloat16)
     square = pltpu.VMEM((ORDER, ORDER), jnp.bfloat16)
+    line = pltpu.VMEM((4, SUB_DEV, SPLIT, BLK), jnp.bfloat16)
+    slots4 = pltpu.VMEM((4, 4, SPLIT, BLK), jnp.bfloat16)
+    slots2 = pltpu.VMEM((2, 2, SPLIT, BLK), jnp.bfloat16)
+    dma = pltpu.SemaphoreType.DMA
     return pl.pallas_call(
         region_kernel,
-        out_shape=jax.ShapeDtypeStruct((SUB_DEV, ORDER, BLK), jnp.bfloat16),
-        in_specs=[pl.BlockSpec(memory_space=pl.ANY), vmem, vmem, smem, smem, smem],
+        out_shape=jax.ShapeDtypeStruct((1, BLK), jnp.float32),
+        in_specs=[hbm, vmem, vmem, smem, smem, smem, smem, smem, smem, hbm],
         out_specs=vmem,
         scratch_shapes=[
             h_buf, h_buf, h_buf, h_buf,
@@ -225,33 +389,18 @@
             pltpu.VMEM((SUB_DEV, ORDER, ORDER), jnp.float32),
             square, square, square,
             pltpu.VMEM((ORDER, BLK), jnp.bfloat16),
-            pltpu.SemaphoreType.DMA((N_SEM,)),
-            pltpu.SemaphoreType.DMA((N_SEM,)),
-            pltpu.SemaphoreType.DMA,
-            pltpu.SemaphoreType.DMA,
+            pltpu.VMEM((OWN_MAX, ORDER, EXT), jnp.bfloat16),
+            line, line, slots4, slots4, slots2, slots2, slots4, slots4,
+            pltpu.VMEM((EXT // BLK, 1, BLK), jnp.float32),
+            pltpu.VMEM((16, 1, BLK), jnp.float32),
+            dma((N_SEM,)), dma((N_SEM,)), dma, dma, dma,
+            dma((8, SUB_DEV)), dma((8, SUB_DEV)), dma((12,)), dma((12,)), dma((11,)), dma((16,)),
         ],
         compiler_params=pltpu.CompilerParams(
-            collective_id=0, has_side_effects=True, vmem_limit_bytes=56 << 20
+            collective_id=0, has_side_effects=True, vmem_limit_bytes=60 << 20
         ),
         name="region",
-    )(h_rows, x_blocks, inverse, same, picks, mu)
-
-
-def from_behind(value, axis, steps):
-    count = lax.axis_size(axis)
-    pairs = [(source, (source + steps) % count) for source in range(count)]
-    return lax.ppermute(value, axis, pairs)
-
-
-def cut_along(value, dim, devices):
-    before, after = (value.shape[:dim], value.shape[dim + 1 :])
-    return jnp.moveaxis(value.reshape(*before, devices, -1, *after), dim, 0)
-
-
-def sum_at_owner(value, axis, dim):
-    parts = cut_along(value, dim, lax.axis_size(axis))
-    arrived = lax.all_to_all(parts, axis, split_axis=0, concat_axis=0, tiled=True)
-    return arrived.sum(axis=0)
+    )(h_rows, x_blocks, inverse, same, picks, mu, which, slots, live, orbitals)
 
 
 def inverse_table(cols):
@@ -265,34 +414,24 @@
 
 
 def on_device(h_rows, x_blocks, x_cols, sub_blocks, owners, shift_mu, orbitals):
-    built = region(
-        h_rows[0], x_blocks[0], inverse_table(x_cols[0]), same_column(x_cols[0]),
-        sub_blocks.reshape(-1), shift_mu,
-    )
     ngrid = lax.axis_size("grid")
     myself = lax.axis_index("grid")
     table = owners[0]
-    targets = lax.dynamic_index_in_dim(table, myself, 0, keepdims=False)
-    hit = table == myself
-    has = jnp.any(hit, axis=1)
-    place = jnp.cumsum(has.astype(jnp.int32)) - 1
+    bricks = jnp.arange(ngrid, dtype=jnp.int32)
+    turn = jnp.arange(SUB_DEV, dtype=jnp.int32)
+    which = jnp.sum(
+        jnp.where(table[:, None, :] == bricks[None, :, None], turn[None, None, :], 0), axis=2
+    )
+    has = jnp.any(table == myself, axis=1)
+    place = jnp.sum((has[None, :] & (bricks[None, :] < bricks[:, None])).astype(jnp.int32), axis=1)
     select = has[None, :] & (place[None, :] == jnp.arange(OWN_MAX, dtype=jnp.int32)[:, None])
-    selint = select.astype(jnp.int32)
-    source = jnp.sum(selint * jnp.arange(ngrid, dtype=jnp.int32)[None, :], axis=1)
-    live = jnp.any(select, axis=1)
-    outgoing = jnp.zeros((ngrid, ORDER, BLK), jnp.bfloat16).at[targets].set(built)
-    incoming = lax.all_to_all(outgoing, "grid", split_axis=0, concat_axis=0, tiled=True)
-    columns = jnp.take(incoming, source, axis=0)
-    phi = orbitals[0, 0]
-    proj = jnp.einsum("tnm,tnx->tmx", columns, phi, preferred_element_type=jnp.float32)
-    values = jnp.sum(proj * phi[:, :BLK, :].astype(jnp.float32), axis=1)
-    window = jnp.sum(jnp.where(live[:, None], values, 0.0), axis=0).reshape(DEPTH + 2 * MARG, PLANE)
-    core = window[MARG : MARG + DEPTH]
-    from_prev = from_behind(window[MARG + DEPTH :], "grid", 1)
-    from_next = from_behind(window[:MARG], "grid", -1)
-    core = core.at[:MARG].add(from_prev)
-    core = core.at[DEPTH - MARG :].add(from_next)
-    return sum_at_owner(core.reshape(1, DEPTH * PLANE), "row", 1)
+    source = jnp.sum(jnp.where(select, bricks[None, :], 0), axis=1)
+    live = jnp.any(select, axis=1).astype(jnp.float32)
+    slots = jnp.stack([source // 4, source % 4], axis=1).reshape(-1)
+    return region(
+        h_rows[0], x_blocks[0], inverse_table(x_cols[0]), same_column(x_cols[0]),
+        sub_blocks.reshape(-1), shift_mu, which.reshape(-1), slots, live, orbitals[0, 0],
+    )
 
 
 def solution(mesh):

time: 171 us -> 131 us (0.77)
  waiting for transfers between devices: 49.7 us -> 0 us
  Pallas kernels: 78.2 us -> 121 us
  starting transfers between devices: 12.6 us -> 0 us
  blocking collectives: 8.59 us -> 0 us
  matrix products: 8.29 us -> 0 us
  local copies, waits for them, and re-layouts: 9.54 us -> 5.03 us
    all_to_all x1 -> x0, waiting for transfers between devices: 48.8 us -> none  [on_device(): lax.all_to_all(outgoing, 'grid', split_axis=0, concat_axis=0, tiled=True)]
    pallas_call x1, Pallas kernels: 78.2 us -> 121 us  [region(): pl.pallas_call(region_kernel, out_shape=jax.ShapeDtypeStruct((1, BLK), jn...]
    all_to_all x1 -> x0, blocking collectives: 8.59 us -> none  [sum_at_owner(): lax.all_to_all(parts, axis, split_axis=0, concat_axis=0, tiled=True)]
    dot_general x1 -> x0, matrix products: 8.29 us -> none  [on_device(): jnp.einsum('tnm,tnx->tmx', columns, phi, preferred_element_type=jnp.float32)]
    all_to_all x1 -> x0, starting transfers between devices: 7.72 us -> none  [on_device(): lax.all_to_all(outgoing, 'grid', split_axis=0, concat_axis=0, tiled=True)]
    ppermute x2 -> x0, starting transfers between devices: 4.85 us -> none  [from_behind(): return lax.ppermute(value, axis, pairs)]
    scatter x1 -> x0, local copies, waits for them, and re-layouts: 2.62 us -> none  [on_device(): jnp.zeros((ngrid, ORDER, BLK), jnp.bfloat16).at[targets].set(built)]
    broadcast_in_dim x1 -> x0, local copies, waits for them, and re-layouts: 2.28 us -> none  [on_device(): jnp.zeros((ngrid, ORDER, BLK), jnp.bfloat16).at[targets].set(built)]
  transfers between devices with their start and end apart: 3 -> 0, of which waited for: 2 -> 0; matrix products, arithmetic and copies ran while one was open for 0% -> 0% of each run, Pallas kernels for 0% -> 0%
where the time goes in v2:
time: 131 us
  Pallas kernels  121 us (92%)
  local copies, waits for them, and re-layouts  5.03 us (4%)
  other arithmetic  3.99 us (3%)
    pallas_call x1, Pallas kernels, region(): pl.pallas_call(region_kernel, out_shape=jax.ShapeDtypeStruct((1, BLK), jn...  121 us

profile of v2, /device:TPU:1, one launch (start us, length us, event | category | flops | bytes accessed | tf_op | source)
XLA Modules:
  0.0 130.9 jit_solution(10768027636000261407)
XLA Ops:
  0.7 0.7 compare_reduce_fusion
  1.4 0.1 convert_reduce_fusion
  1.5 0.1 fusion.2
  1.6 0.1 select_reduce_fusion.2
  1.7 0.6 convert_element_type.16.live_in
  2.3 0.8 select_reduce_fusion.1
  3.1 0.7 reduce.2
  3.8 0.6 reshape.123.picks
  4.4 0.7 copy.17
  5.1 0.1 copy.12
  5.2 0.7 reshape.125.slots_in
  5.8 0.1 select_reduce_fusion
  5.9 0.7 reshape.124.which_in
  6.5 0.6 scatter.4.inv_in
  7.1 0.8 compare_convert_fusion
  8.0 0.6 reshape.126.same_in
  8.6 121.2 %region.1 = f32[1,128]{1,0:T(1,128)} custom-call(bf16[256,2048]{1,0:T(8,128)(2,1)} %bitcast.25, bf16[2,8,128,128]{3,2,1,0:T(8,128)(2,1)} %bitcast.26, s32[2,8,128]{2,1,0:T(8,128)} %scatter.4.inv_in, f32[128]{0:T(128)} %reshape.126.same_in, s32[18]{0:T(128)} %reshape.123.picks, f32[1]{0:T(128)S(6)} %copy.19.mu_in, s32[256]{0:T(256)} %reshape.124.which_in, ...), custom_call_target="tpu_custom_call" | custom-call | tf_op jit(solution)/shard_map/region/pallas_call | solution.py:377
  129.7 1.1 copy.20
  (3 shorter events, 0.0 us)

commit v3 on v2

v3 whole, which is shorter than its diff:
```python
import jax
import jax.numpy as jnp
from jax import lax
from jax.experimental import pallas as pl
from jax.experimental.pallas import tpu as pltpu
from jax.sharding import PartitionSpec as P

BLK = 128
SUB_BLK = 6
NZ = 8
SUB_DEV = 3
OWN_MAX = 6
PLANE = 256
DEPTH = 4
MARG = 1
ORDER = 768
KB = 16
NREG = 2048
HALF = 64
TILE = 256
SPLIT = 384
EXT = 1536

X_DN, X_UP, X_SIB, X_FAR_A, X_FAR_B, X_SDN, X_SUP, X_SFAR_A, X_SFAR_B = range(9)
T_DN, T_UP, T_SIB, T_FAR, T_SDN, T_SUP, T_SFAR = range(9, 16)
H_DN, H_UP, H_SIB, H_SDN, H_SUP, H_FAR_A, H_FAR_B, H_SFAR_A, H_SFAR_B = range(16, 34, 2)
N_SEM = 34


def eye_like(rows, cols, first_row):
    row = lax.broadcasted_iota(jnp.int32, (rows, cols), 0) + first_row
    col = lax.broadcasted_iota(jnp.int32, (rows, cols), 1)
    return row == col


def region_kernel(
    h_in, x_in, cols_in, picks, owners, mu_in, phi_in, out,
    h_own, h_dn, h_up, h_far_a, h_far_b, x_all, table, table_s, lhs, rhs, total, w, y0, z1, y1,
    phi, line_x, line_z, pack_x, pack_z, pass_x, pass_z, got_x, got_z, column, pieces, sums,
    send_sem, recv_sem, own_sem, table_sem, phi_sem,
    line_send, line_recv, swap_send, swap_recv, sum_send, sum_recv,
):
    r = lax.axis_index("row")
    g = lax.axis_index("grid")
    gz = g // 4
    gx = g - 4 * gz
    y = r // 2
    core = r - 2 * y
    sib = 2 * y + 1 - core
    y_up, y_dn, y_far = lax.rem(y + 1, 4), lax.rem(y + 3, 4), lax.rem(y + 2, 4)
    up, dn = 2 * y_up + core, 2 * y_dn + core
    x_next = 4 * gz + lax.rem(gx + 1, 4)
    x_prev = 4 * gz + lax.rem(gx + 3, 4)
    z_next = 4 * lax.rem(gz + 1, 4) + gx
    z_prev = 4 * lax.rem(gz + 3, 4) + gx
    brick_next = lax.rem(g + 1, 16)
    brick_prev = lax.rem(g + 15, 16)

    for b in range(KB):
        pltpu.make_async_copy(
            h_in.at[:, b * BLK : (b + 1) * BLK], h_own.at[core, b], own_sem
        ).start()
    sums[...] = jnp.zeros_like(sums)
    barrier = pltpu.get_barrier_semaphore()

    def greet(row, grid):
        pl.semaphore_signal(
            barrier, inc=1, device_id=(row, grid), device_id_type=pl.DeviceIdType.MESH
        )

    for step in range(1, 8):
        greet(lax.rem(r + step, 8), g)
    for other in (x_next, x_prev, z_next, z_prev):
        greet(r, other)

    @pl.when(r < 2)
    def _():
        for row in range(8):
            greet(row, brick_prev)

    @pl.when(r >= 6)
    def _():
        for row in range(8):
            greet(row, brick_next)

    copies = {}

    def send(slot, src, dst, device):
        copy = pltpu.make_async_remote_copy(
            src_ref=src, dst_ref=dst, send_sem=send_sem.at[slot], recv_sem=recv_sem.at[slot],
            device_id=(device, g), device_id_type=pl.DeviceIdType.MESH,
        )
        copy.start()
        copies[slot] = copy

    def half(ref, which):
        return ref.at[core, pl.ds(0, KB), pl.ds(which * BLK, BLK)]

    def far_part(ref, which):
        return ref.at[core, pl.ds(0, KB), pl.ds(which * HALF, HALF)]

    def near_part(ref, block, which):
        return ref.at[core, pl.ds(0, KB), pl.ds(block * BLK + which * HALF, HALF)]

    def x_rows(origin):
        return x_all.at[pl.ds(2 * origin, 2), pl.ds(0, NZ)]

    def x_row(origin, i):
        return x_all.at[2 * origin + i, pl.ds(0, NZ)]

    def t_rows(origin):
        return table.at[pl.ds(2 * origin, 2)]

    pltpu.make_async_copy(h_own.at[core], h_own.at[core], own_sem).wait()
    pl.semaphore_wait(barrier, 15)
    for slot, ref, device in ((H_DN, h_dn, up), (H_UP, h_up, dn), (H_SIB, h_own, sib)):
        send(slot, half(h_own, 0), half(ref, 0), device)

    lane = lax.broadcasted_iota(jnp.int32, (8, BLK), 1)
    for i in range(2):
        first = jnp.full((8, BLK), NZ, jnp.int32)
        for z in reversed(range(NZ)):
            first = jnp.where(lane == cols_in[i, z], z, first)
        table[2 * r + i] = first
        for z in range(NZ):
            block = x_in[i, z].astype(jnp.float32)
            for v in range(z + 1, NZ):
                same = (cols_in[i, v] == cols_in[i, z]).astype(jnp.int32).astype(jnp.float32)
                block += x_in[i, v].astype(jnp.float32) * same
            x_all[2 * r + i, z] = block.astype(jnp.bfloat16)
    for slot, device in ((X_DN, up), (X_UP, dn), (X_SIB, sib)):
        send(slot, x_rows(r), x_rows(r), device)
    for slot, device in ((T_DN, up), (T_UP, dn), (T_SIB, sib)):
        send(slot, t_rows(r), t_rows(r), device)
    for slot, ref, device in ((H_DN, h_dn, up), (H_UP, h_up, dn), (H_SIB, h_own, sib)):
        send(slot + 1, half(h_own, 1), half(ref, 1), device)
    phi_copy = pltpu.make_async_copy(phi_in, phi, phi_sem)
    phi_copy.start()
    for i in range(KB):
        x_all[i, NZ] = jnp.zeros((BLK, BLK), jnp.bfloat16)

    def item_for(source, owner):
        found = sum(k * (owners[source, k] == owner).astype(jnp.int32) for k in range(1, SUB_DEV))
        return jnp.minimum(found, SUB_DEV - 1)

    count = jnp.int32(0)
    slot_source = [jnp.int32(0)] * OWN_MAX
    for source in range(16):
        has = sum((owners[source, k] == g).astype(jnp.int32) for k in range(SUB_DEV))
        has = jnp.minimum(has, 1)
        for t in range(OWN_MAX):
            slot_source[t] += source * has * (count == t).astype(jnp.int32)
        count += has

    def relay_h(block):
        far, far_ref = (H_FAR_A, h_far_a) if block == 0 else (H_FAR_B, h_far_b)
        copies[H_DN + block].wait_recv()
        send(far, near_part(h_dn, block, 0), far_part(far_ref, 0), up)
        send(H_SDN + block, half(h_dn, block), half(h_dn, block), sib)
        copies[H_UP + block].wait_recv()
        send(far + 1, near_part(h_up, block, 1), far_part(far_ref, 1), dn)
        send(H_SUP + block, half(h_up, block), half(h_up, block), sib)

    far = 2 * y_far + core
    copies[X_DN].wait_recv()
    send(X_FAR_A, x_row(dn, 0), x_row(dn, 0), up)
    send(X_SDN, x_rows(dn), x_rows(dn), sib)
    copies[X_UP].wait_recv()
    send(X_FAR_B, x_row(up, 1), x_row(up, 1), dn)
    send(X_SUP, x_rows(up), x_rows(up), sib)
    copies[T_DN].wait_recv()
    send(T_FAR, t_rows(dn), t_rows(dn), up)
    send(T_SDN, t_rows(dn), t_rows(dn), sib)
    copies[T_UP].wait_recv()
    send(T_SUP, t_rows(up), t_rows(up), sib)
    relay_h(0)
    copies[X_FAR_A].wait_recv()
    send(X_SFAR_A, x_row(far, 0), x_row(far, 0), sib)
    copies[X_FAR_B].wait_recv()
    send(X_SFAR_B, x_row(far, 1), x_row(far, 1), sib)
    copies[T_FAR].wait_recv()
    send(T_SFAR, t_rows(far), t_rows(far), sib)

    for slot in (X_SIB, X_SDN, X_SUP, X_SFAR_A, X_SFAR_B, T_SIB, T_SDN, T_SUP, T_SFAR):
        copies[slot].wait_recv()
    table_copy = pltpu.make_async_copy(table, table_s, table_sem)
    table_copy.start()
    table_copy.wait()

    def pick_blocks(k, h_ref, chip, blocks):
        for b in range(SUB_BLK):
            pick = picks[k, b]
            rows = slice(b * BLK, (b + 1) * BLK)
            for c in range(2):
                for n, block in enumerate(blocks):
                    z = table_s[pick, 0, 4 * chip + 2 * c + block]
                    at = (c * len(blocks) + n) * BLK
                    lhs[rows, at : at + BLK] = x_all[pick, z]
                depth = len(blocks) * BLK
                rhs[c * depth : (c + 1) * depth, rows] = h_ref[c, pick]

    def accumulate(h_ref, chip, blocks, first):
        depth = 2 * len(blocks) * BLK

        def one(k, carry):
            pick_blocks(k, h_ref, chip, blocks)
            part = jnp.dot(lhs[:, :depth], rhs[:depth, :], preferred_element_type=jnp.float32)
            if first:
                total[k] = part
            else:
                total[k] += part
            return carry

        lax.fori_loop(0, SUB_DEV, one, 0)

    copies[H_SIB].wait_recv()
    copies[H_SIB + 1].wait_recv()
    accumulate(h_own, y, (0, 1), True)
    relay_h(1)
    for ref, slot, chip in ((h_dn, H_SDN, y_dn), (h_up, H_SUP, y_up)):
        copies[slot].wait_recv()
        copies[slot + 1].wait_recv()
        accumulate(ref, chip, (0, 1), False)
    for far, passed, ref in ((H_FAR_A, H_SFAR_A, h_far_a), (H_FAR_B, H_SFAR_B, h_far_b)):
        for which in range(2):
            copies[far + which].wait_recv()
            send(passed + which, far_part(ref, which), far_part(ref, which), sib)
        for which in range(2):
            copies[passed + which].wait_recv()
        if far == H_FAR_A:
            accumulate(ref, y_far, (0,), False)

    mu = mu_in[0]

    def line_copy(way, k):
        line, me, before, after = (
            (line_x, gx, x_prev, x_next) if way < 4 else (line_z, gz, z_prev, z_next)
        )
        kind = way % 4
        source = lax.rem(me + (0, 0, 3, 1)[kind], 4)
        rows = (pl.ds(0, SPLIT), pl.ds(0, SPLIT), pl.ds(0, SPLIT // 2), pl.ds(SPLIT // 2, SPLIT // 2))
        part = line.at[source, k, rows[kind]]
        return pltpu.make_async_remote_copy(
            src_ref=part, dst_ref=part,
            send_sem=line_send.at[way, k], recv_sem=line_recv.at[way, k],
            device_id=(r, (after, before, after, before)[kind]),
            device_id_type=pl.DeviceIdType.MESH,
        )

    def pass_on(k):
        for first in (0, 4):
            line_copy(first, k).wait_recv()
            line_copy(first + 2, k).start()
            line_copy(first + 1, k).wait_recv()
            line_copy(first + 3, k).start()

    def sign(k, carry):
        pick_blocks(k, h_far_b, y_far, (1,))
        norm = jnp.zeros((1, TILE), jnp.float32)
        for n in range(3):
            cols = slice(n * TILE, (n + 1) * TILE)
            part = jnp.dot(
                lhs[:, :TILE], rhs[:TILE, cols], preferred_element_type=jnp.float32
            )
            mat = (total[k, :, cols] + part).astype(jnp.bfloat16).astype(jnp.float32)
            shifted = mat - jnp.where(eye_like(ORDER, TILE, -n * TILE), mu, 0.0)
            norm += jnp.sum(shifted * shifted, axis=0, keepdims=True)
            w[:, cols] = shifted.astype(jnp.bfloat16)
        square_scale = jnp.sum(norm, axis=1, keepdims=True) / ORDER + 1e-06
        scale_y = 0.25 / square_scale
        scale_z = 0.25 / jnp.sqrt(square_scale)
        for n in range(3):
            cols = slice(n * TILE, (n + 1) * TILE)
            square = jnp.dot(w[...], w[:, cols], preferred_element_type=jnp.float32)
            diag = jnp.where(eye_like(ORDER, TILE, -n * TILE), 3.0, 0.0)
            y0[:, cols] = (diag - scale_y * square).astype(jnp.bfloat16)
        for n in range(3):
            cols = slice(n * TILE, (n + 1) * TILE)
            step = jnp.dot(w[...], y0[:, cols], preferred_element_type=jnp.float32)
            z1[:, cols] = (scale_z * step).astype(jnp.bfloat16)
        square = jnp.dot(z1[...], z1[:, :BLK], preferred_element_type=jnp.float32)
        eye = eye_like(ORDER, BLK, 0)
        y1[...] = (jnp.where(eye, 3.0, 0.0) - square).astype(jnp.bfloat16)
        last = 0.5 * jnp.dot(z1[...], y1[...], preferred_element_type=jnp.float32)
        columns = (0.5 * (jnp.where(eye, 1.0, 0.0) - last)).astype(jnp.bfloat16)
        line_x[gx, k] = columns[:SPLIT]
        line_z[gz, k] = columns[SPLIT:]
        for way in (0, 1, 4, 5):
            line_copy(way, k).start()

        @pl.when(k > 0)
        def _():
            pass_on(k - 1)

        return carry

    lax.fori_loop(0, SUB_DEV, sign, 0)
    pass_on(SUB_DEV - 1)
    for k in range(SUB_DEV):
        for way in (2, 3, 6, 7):
            line_copy(way, k).wait_recv()

    for s in range(4):
        for step in (2, 1, 3):
            to_z = lax.rem(gz + step, 4)
            pack_x[step, s] = line_x[s, item_for(4 * gz + s, 4 * to_z + gx)]
            to_x = lax.rem(gx + step, 4)
            pack_z[step, s] = line_z[s, item_for(4 * s + gx, 4 * gz + to_x)]

    def swap(slot, src, dst, device):
        return pltpu.make_async_remote_copy(
            src_ref=src, dst_ref=dst,
            send_sem=swap_send.at[slot], recv_sem=swap_recv.at[slot],
            device_id=(r, device), device_id_type=pl.DeviceIdType.MESH,
        )

    def swaps(base, pack, passed, got, me, before, after):
        first, last = pl.ds(0, 2), pl.ds(2, 2)
        away = [
            swap(base, pack.at[2, first], passed.at[0], after),
            swap(base + 1, pack.at[2, last], passed.at[1], before),
            swap(base + 2, pack.at[1], got.at[me], after),
            swap(base + 3, pack.at[3], got.at[me], before),
        ]
        far = [
            swap(base + 4, passed.at[0], got.at[lax.rem(me + 3, 4), first], after),
            swap(base + 5, passed.at[1], got.at[lax.rem(me + 1, 4), last], before),
        ]
        return away, far

    away_x, far_x = swaps(0, pack_x, pass_x, got_x, gz, z_prev, z_next)
    away_z, far_z = swaps(6, pack_z, pass_z, got_z, gx, x_prev, x_next)
    for one in (*away_x, *away_z):
        one.start()
    for s in range(4):
        got_x[gz, s] = line_x[s, item_for(4 * gz + s, g)]
        got_z[gx, s] = line_z[s, item_for(4 * s + gx, g)]
    for i in range(2):
        for away, far in ((away_x, far_x), (away_z, far_z)):
            away[i].wait_recv()
            far[i].start()
    for one in (*away_x[2:], *away_z[2:], *far_x, *far_z):
        one.wait_recv()
    phi_copy.wait()

    across = (((0,), (0,)), ((), ()))
    window = jnp.zeros((1, EXT), jnp.float32)
    for t in range(OWN_MAX):
        from_z = slot_source[t] // 4
        from_x = slot_source[t] - 4 * from_z
        column[:SPLIT] = got_x[from_z, from_x]
        column[SPLIT:] = got_z[from_x, from_z]
        proj = lax.dot_general(column[...], phi[t], across, preferred_element_type=jnp.float32)
        values = jnp.sum(proj * phi[t, :BLK].astype(jnp.float32), axis=0, keepdims=True)
        window += values * (count > t).astype(jnp.int32).astype(jnp.float32)
    for i in range(EXT // BLK):
        pieces[i] = window[:, i * BLK : (i + 1) * BLK]

    def give(slot, piece, place, row, grid):
        copy = pltpu.make_async_remote_copy(
            src_ref=pieces.at[piece], dst_ref=sums.at[place],
            send_sem=sum_send.at[slot], recv_sem=sum_recv.at[place],
            device_id=(row, grid), device_id_type=pl.DeviceIdType.MESH,
        )
        copy.start()
        return copy

    given = []
    for row in range(2):
        given.append(give(7 + row, 10 + row, 8 + r, row, brick_next))
        given.append(give(9 + row, row, 8 + r, 6 + row, brick_prev))
    for step in range(1, 8):
        row = lax.rem(r + step, 8)
        given.append(give(step - 1, 2 + row, r, row, g))
    sums[r] = pieces[2 + r]

    def arrived(place):
        pltpu.make_async_copy(sums.at[place], sums.at[place], sum_recv.at[place]).wait()

    for step in range(1, 8):
        arrived(lax.rem(r + step, 8))

    @pl.when((r < 2) | (r >= 6))
    def _():
        for row in range(8):
            arrived(8 + row)

    out[...] = jnp.sum(sums[...], axis=0)
    for copy in (*copies.values(), *away_x, *away_z, *far_x, *far_z, *given):
        copy.wait_send()
    for k in range(SUB_DEV):
        for way in range(8):
            line_copy(way, k).wait_send()


def region(h_rows, x_blocks, x_cols, picks, owners, mu, orbitals):
    vmem = pl.BlockSpec(memory_space=pltpu.VMEM)
    smem = pl.BlockSpec(memory_space=pltpu.SMEM)
    hbm = pl.BlockSpec(memory_space=pl.ANY)
    h_buf = pltpu.VMEM((2, KB, 2 * BLK, BLK), jnp.bfloat16)
    h_far = pltpu.VMEM((2, KB, BLK, BLK), jnp.bfloat16)
    square = pltpu.VMEM((ORDER, ORDER), jnp.bfloat16)
    columns = pltpu.VMEM((ORDER, BLK), jnp.bfloat16)
    line = pltpu.VMEM((4, SUB_DEV, SPLIT, BLK), jnp.bfloat16)
    slots4 = pltpu.VMEM((4, 4, SPLIT, BLK), jnp.bfloat16)
    slots2 = pltpu.VMEM((2, 2, SPLIT, BLK), jnp.bfloat16)
    dma = pltpu.SemaphoreType.DMA
    return pl.pallas_call(
        region_kernel,
        out_shape=jax.ShapeDtypeStruct((1, BLK), jnp.float32),
        in_specs=[hbm, vmem, smem, smem, smem, smem, hbm],
        out_specs=vmem,
        scratch_shapes=[
            h_buf, h_buf, h_buf, h_far, h_far,
            pltpu.VMEM((KB, NZ + 1, BLK, BLK), jnp.bfloat16),
            pltpu.VMEM((KB, 8, BLK), jnp.int32),
            pltpu.SMEM((KB, 8, BLK), jnp.int32),
            pltpu.VMEM((ORDER, 4 * BLK), jnp.bfloat16),
            pltpu.VMEM((4 * BLK, ORDER), jnp.bfloat16),
            pltpu.VMEM((SUB_DEV, ORDER, ORDER), jnp.float32),
            square, square, square, columns,
            pltpu.VMEM((OWN_MAX, ORDER, EXT), jnp.bfloat16),
            line, line, slots4, slots4, slots2, slots2, slots4, slots4, columns,
            pltpu.VMEM((EXT // BLK, 1, BLK), jnp.float32),
            pltpu.VMEM((16, 1, BLK), jnp.float32),
            dma((N_SEM,)), dma((N_SEM,)), dma, dma, dma,
            dma((8, SUB_DEV)), dma((8, SUB_DEV)), dma((12,)), dma((12,)), dma((11,)), dma((16,)),
        ],
        compiler_params=pltpu.CompilerParams(
            collective_id=0, has_side_effects=True, vmem_limit_bytes=60 << 20
        ),
        name="region",
    )(h_rows, x_blocks, x_cols, picks, owners, mu, orbitals)


def on_device(h_rows, x_blocks, x_cols, sub_blocks, owners, shift_mu, orbitals):
    return region(
        h_rows[0], x_blocks[0], x_cols[0], sub_blocks[0, 0], owners[0], shift_mu, orbitals[0, 0]
    )


def solution(mesh):
    in_specs = (
        P("grid", "row", None),
        P("grid", "row", None, None, None),
        P("grid", "row", None),
        P("row", "grid", None, None),
        P("row", None, None),
        P(),
        P("row", "grid", None, None, None),
    )
    out_specs = P("grid", "row")
    return jax.shard_map(
        on_device, mesh=mesh, in_specs=in_specs, out_specs=out_specs, check_vma=False
    )
```

time: 131 us -> 122 us (0.931)
  Pallas kernels: 121 us -> 117 us
  other arithmetic: 3.99 us -> 0 us
    pallas_call x1, Pallas kernels: 121 us -> 117 us  [region(): pl.pallas_call(region_kernel, out_shape=jax.ShapeDtypeStruct((1, BLK), jn...]
    reshape x3 -> x0, local copies, waits for them, and re-layouts: 1.93 us -> none  [the longest x1 0.66 us: on_device(): which.reshape(-1)]
    convert_element_type x2 -> x0, other arithmetic: 1.37 us -> none  [the longest x1 0.82 us: same_column(): (cols[:, :, None] == cols[:, None, :]).astype(jnp.float32).reshape(-1)]
    squeeze x0 -> x1, local copies, waits for them, and re-layouts: none -> 1.35 us  [on_device(): owners[0]]
where the time goes in v3:
time: 122 us; the launch traced here: 121 us
  Pallas kernels  117 us (96%)
  local copies, waits for them, and re-layouts  3.76 us (3%)
    pallas_call x1, Pallas kernels, region(): pl.pallas_call(region_kernel, out_shape=jax.ShapeDtypeStruct((1, BLK), jn...  117 us

profile of v3, /device:TPU:1, one launch (start us, length us, event | category | flops | bytes accessed | tf_op | source)
XLA Modules:
  0.0 121.4 jit_solution(6192343660690992321)
XLA Ops:
  0.7 1.3 %copy.12 = s32[1,1,3,6]{3,2,1,0:T(4,128)} copy(s32[1,1,3,6]{3,1,2,0:T(1,128)} %param.10) | data formatting | bytes 144
  1.9 1.4 %copy.9 = s32[1,16,3]{2,1,0:T(8,128)} copy(s32[1,16,3]{1,0,2:T(1,128)} %param.11) | data formatting | bytes 384 | tf_op jit(solution)/shard_map/squeeze | solution.py:438
  3.3 117.0 %region.1 = f32[1,128]{1,0:T(1,128)} custom-call(bf16[256,2048]{1,0:T(8,128)(2,1)} %bitcast.9, bf16[2,8,128,128]{3,2,1,0:T(8,128)(2,1)} %bitcast.10, s32[2,8]{1,0:T(2,128)} %bitcast.13, s32[3,6]{1,0:T(4,128)} %bitcast.12, s32[16,3]{1,0:T(8,128)} %bitcast.11, f32[1]{0:T(128)S(6)} %copy.14.mu_in, bf16[6,768,1536]{2,1,0:T(8,128)(2,1)} %bitcast.8), custom_call_target="tpu_custom_call" | custom-call | tf_op jit(solution)/shard_map/region/pallas_call | solution.py:408
  120.3 1.1 copy.15

commit v4 on v3

--- a/solution.py
+++ b/solution.py
@@ -232,27 +232,84 @@
 
     mu = mu_in[0]
 
-    def line_copy(way, k):
-        line, me, before, after = (
-            (line_x, gx, x_prev, x_next) if way < 4 else (line_z, gz, z_prev, z_next)
-        )
-        kind = way % 4
-        source = lax.rem(me + (0, 0, 3, 1)[kind], 4)
-        rows = (pl.ds(0, SPLIT), pl.ds(0, SPLIT), pl.ds(0, SPLIT // 2), pl.ds(SPLIT // 2, SPLIT // 2))
-        part = line.at[source, k, rows[kind]]
-        return pltpu.make_async_remote_copy(
-            src_ref=part, dst_ref=part,
-            send_sem=line_send.at[way, k], recv_sem=line_recv.at[way, k],
-            device_id=(r, (after, before, after, before)[kind]),
-            device_id_type=pl.DeviceIdType.MESH,
-        )
+    class Way:
+        def __init__(self, line, me, prev, nxt, swap_me, swap_prev, swap_nxt, x_first, bufs, base):
+            self.own, self.nxt, self.prev, self.far = line
+            self.me, self.to_prev, self.to_nxt = me, prev, nxt
+            self.swap_me, self.swap_prev, self.swap_nxt = swap_me, swap_prev, swap_nxt
+            self.x_first = x_first
+            self.pack, self.passed, self.got = bufs
+            self.base = base
+
+        def grid(self, line_place, swap_place):
+            if self.x_first:
+                return 4 * swap_place + line_place
+            return 4 * line_place + swap_place
+
+        def line_copy(self, kind, k):
+            rows = (pl.ds(0, SPLIT), pl.ds(0, SPLIT), pl.ds(0, SPLIT // 2), pl.ds(SPLIT // 2, SPLIT // 2))
+            src = (self.own, self.own, self.prev, self.nxt)[kind]
+            dst = (self.prev, self.nxt, self.far, self.far)[kind]
+            slot = 4 * self.base + kind
+            return pltpu.make_async_remote_copy(
+                src_ref=src.at[k, rows[kind]], dst_ref=dst.at[k, rows[kind]],
+                send_sem=line_send.at[slot, k], recv_sem=line_recv.at[slot, k],
+                device_id=(r, (self.to_nxt, self.to_prev, self.to_nxt, self.to_prev)[kind]),
+                device_id_type=pl.DeviceIdType.MESH,
+            )
+
+        def fill(self, slot):
+            buf, place = (
+                (self.own, 0), (self.nxt, 1), (self.prev, 3), (self.far, 2)
+            )[slot]
+            source = self.grid(lax.rem(self.me + place, 4), self.swap_me)
+            for step in (2, 1, 3):
+                owner = self.grid(self.me, lax.rem(self.swap_me + step, 4))
+                self.pack[step - 1, slot] = buf[item_for(source, owner)]
+            self.got[0, slot] = buf[item_for(source, g)]
+
+        def swap(self, group, kind):
+            slots = (pl.ds(0, 1), pl.ds(1, 2), pl.ds(3, 1))[group]
+            top, low = pl.ds(0, SPLIT // 2), pl.ds(SPLIT // 2, SPLIT // 2)
+            src, dst, device = (
+                (self.pack.at[1, slots, top], self.passed.at[0, slots], self.swap_nxt),
+                (self.pack.at[1, slots, low], self.passed.at[1, slots], self.swap_prev),
+                (self.pack.at[0, slots], self.got.at[3, slots], self.swap_nxt),
+                (self.pack.at[2, slots], self.got.at[1, slots], self.swap_prev),
+                (self.passed.at[0, slots], self.got.at[2, slots, top], self.swap_nxt),
+                (self.passed.at[1, slots], self.got.at[2, slots, low], self.swap_prev),
+            )[kind]
+            slot = 6 * (3 * self.base + group) + kind
+            return pltpu.make_async_remote_copy(
+                src_ref=src, dst_ref=dst,
+                send_sem=swap_send.at[slot], recv_sem=swap_recv.at[slot],
+                device_id=(r, device), device_id_type=pl.DeviceIdType.MESH,
+            )
+
+    along_x = Way(line_x, gx, x_prev, x_next, gz, z_prev, z_next, True, (pack_x, pass_x, got_x), 0)
+    along_z = Way(line_z, gz, z_prev, z_next, gx, x_prev, x_next, False, (pack_z, pass_z, got_z), 1)
+    ways = (along_x, along_z)
 
     def pass_on(k):
-        for first in (0, 4):
-            line_copy(first, k).wait_recv()
-            line_copy(first + 2, k).start()
-            line_copy(first + 1, k).wait_recv()
-            line_copy(first + 3, k).start()
+        for way in ways:
+            way.line_copy(0, k).wait_recv()
+            way.line_copy(2, k).start()
+            way.line_copy(1, k).wait_recv()
+            way.line_copy(3, k).start()
+
+    def swap_out(group, slots):
+        for way in ways:
+            for slot in slots:
+                way.fill(slot)
+        for kind in range(4):
+            for way in ways:
+                way.swap(group, kind).start()
+
+    def swap_on(group):
+        for kind in range(2):
+            for way in ways:
+                way.swap(group, kind).wait_recv()
+                way.swap(group, kind + 4).start()
 
     def sign(k, carry):
         pick_blocks(k, h_far_b, y_far, (1,))
@@ -283,10 +340,11 @@
         y1[...] = (jnp.where(eye, 3.0, 0.0) - square).astype(jnp.bfloat16)
         last = 0.5 * jnp.dot(z1[...], y1[...], preferred_element_type=jnp.float32)
         columns = (0.5 * (jnp.where(eye, 1.0, 0.0) - last)).astype(jnp.bfloat16)
-        line_x[gx, k] = columns[:SPLIT]
-        line_z[gz, k] = columns[SPLIT:]
-        for way in (0, 1, 4, 5):
-            line_copy(way, k).start()
+        along_x.own[k] = columns[:SPLIT]
+        along_z.own[k] = columns[SPLIT:]
+        for way in ways:
+            way.line_copy(0, k).start()
+            way.line_copy(1, k).start()
 
         @pl.when(k > 0)
         def _():
@@ -295,61 +353,34 @@
         return carry
 
     lax.fori_loop(0, SUB_DEV, sign, 0)
+    swap_out(0, (0,))
     pass_on(SUB_DEV - 1)
+    swap_out(1, (1, 2))
+    swap_on(0)
     for k in range(SUB_DEV):
-        for way in (2, 3, 6, 7):
-            line_copy(way, k).wait_recv()
-
-    for s in range(4):
-        for step in (2, 1, 3):
-            to_z = lax.rem(gz + step, 4)
-            pack_x[step, s] = line_x[s, item_for(4 * gz + s, 4 * to_z + gx)]
-            to_x = lax.rem(gx + step, 4)
-            pack_z[step, s] = line_z[s, item_for(4 * s + gx, 4 * gz + to_x)]
-
-    def swap(slot, src, dst, device):
-        return pltpu.make_async_remote_copy(
-            src_ref=src, dst_ref=dst,
-            send_sem=swap_send.at[slot], recv_sem=swap_recv.at[slot],
-            device_id=(r, device), device_id_type=pl.DeviceIdType.MESH,
-        )
-
-    def swaps(base, pack, passed, got, me, before, after):
-        first, last = pl.ds(0, 2), pl.ds(2, 2)
-        away = [
-            swap(base, pack.at[2, first], passed.at[0], after),
-            swap(base + 1, pack.at[2, last], passed.at[1], before),
-            swap(base + 2, pack.at[1], got.at[me], after),
-            swap(base + 3, pack.at[3], got.at[me], before),
-        ]
-        far = [
-            swap(base + 4, passed.at[0], got.at[lax.rem(me + 3, 4), first], after),
-            swap(base + 5, passed.at[1], got.at[lax.rem(me + 1, 4), last], before),
-        ]
-        return away, far
-
-    away_x, far_x = swaps(0, pack_x, pass_x, got_x, gz, z_prev, z_next)
-    away_z, far_z = swaps(6, pack_z, pass_z, got_z, gx, x_prev, x_next)
-    for one in (*away_x, *away_z):
-        one.start()
-    for s in range(4):
-        got_x[gz, s] = line_x[s, item_for(4 * gz + s, g)]
-        got_z[gx, s] = line_z[s, item_for(4 * s + gx, g)]
-    for i in range(2):
-        for away, far in ((away_x, far_x), (away_z, far_z)):
-            away[i].wait_recv()
-            far[i].start()
-    for one in (*away_x[2:], *away_z[2:], *far_x, *far_z):
-        one.wait_recv()
+        for way in ways:
+            way.line_copy(2, k).wait_recv()
+            way.line_copy(3, k).wait_recv()
+    swap_out(2, (3,))
+    swap_on(1)
+    swap_on(2)
+    for group in range(3):
+        for kind in range(2, 6):
+            for way in ways:
+                way.swap(group, kind).wait_recv()
     phi_copy.wait()
+
+    def slot_of(place):
+        return place + (place == 2).astype(jnp.int32) - (place == 3).astype(jnp.int32)
 
     across = (((0,), (0,)), ((), ()))
     window = jnp.zeros((1, EXT), jnp.float32)
     for t in range(OWN_MAX):
         from_z = slot_source[t] // 4
-        from_x = slot_source[t] - 4 * from_z
-        column[:SPLIT] = got_x[from_z, from_x]
-        column[SPLIT:] = got_z[from_x, from_z]
+        from_x = lax.rem(slot_source[t] - 4 * from_z + 4 - gx, 4)
+        from_z = lax.rem(from_z + 4 - gz, 4)
+        column[:SPLIT] = got_x[from_z, slot_of(from_x)]
+        column[SPLIT:] = got_z[from_x, slot_of(from_z)]
         proj = lax.dot_general(column[...], phi[t], across, preferred_element_type=jnp.float32)
         values = jnp.sum(proj * phi[t, :BLK].astype(jnp.float32), axis=0, keepdims=True)
         window += values * (count > t).astype(jnp.int32).astype(jnp.float32)
@@ -386,11 +417,15 @@
             arrived(8 + row)
 
     out[...] = jnp.sum(sums[...], axis=0)
-    for copy in (*copies.values(), *away_x, *away_z, *far_x, *far_z, *given):
+    for copy in (*copies.values(), *given):
         copy.wait_send()
-    for k in range(SUB_DEV):
-        for way in range(8):
-            line_copy(way, k).wait_send()
+    for way in ways:
+        for kind in range(4):
+            for k in range(SUB_DEV):
+                way.line_copy(kind, k).wait_send()
+        for kind in range(6):
+            for group in range(3):
+                way.swap(group, kind).wait_send()
 
 
 def region(h_rows, x_blocks, x_cols, picks, owners, mu, orbitals):
@@ -401,9 +436,10 @@
     h_far = pltpu.VMEM((2, KB, BLK, BLK), jnp.bfloat16)
     square = pltpu.VMEM((ORDER, ORDER), jnp.bfloat16)
     columns = pltpu.VMEM((ORDER, BLK), jnp.bfloat16)
-    line = pltpu.VMEM((4, SUB_DEV, SPLIT, BLK), jnp.bfloat16)
+    line = [pltpu.VMEM((SUB_DEV, SPLIT, BLK), jnp.bfloat16)] * 4
+    pack = pltpu.VMEM((3, 4, SPLIT, BLK), jnp.bfloat16)
     slots4 = pltpu.VMEM((4, 4, SPLIT, BLK), jnp.bfloat16)
-    slots2 = pltpu.VMEM((2, 2, SPLIT, BLK), jnp.bfloat16)
+    passed = pltpu.VMEM((2, 4, SPLIT // 2, BLK), jnp.bfloat16)
     dma = pltpu.SemaphoreType.DMA
     return pl.pallas_call(
         region_kernel,
@@ -420,11 +456,11 @@
             pltpu.VMEM((SUB_DEV, ORDER, ORDER), jnp.float32),
             square, square, square, columns,
             pltpu.VMEM((OWN_MAX, ORDER, EXT), jnp.bfloat16),
-            line, line, slots4, slots4, slots2, slots2, slots4, slots4, columns,
+            line, line, pack, pack, passed, passed, slots4, slots4, columns,
             pltpu.VMEM((EXT // BLK, 1, BLK), jnp.float32),
             pltpu.VMEM((16, 1, BLK), jnp.float32),
             dma((N_SEM,)), dma((N_SEM,)), dma, dma, dma,
-            dma((8, SUB_DEV)), dma((8, SUB_DEV)), dma((12,)), dma((12,)), dma((11,)), dma((16,)),
+            dma((8, SUB_DEV)), dma((8, SUB_DEV)), dma((36,)), dma((36,)), dma((11,)), dma((16,)),
         ],
         compiler_params=pltpu.CompilerParams(
             collective_id=0, has_side_effects=True, vmem_limit_bytes=60 << 20

time: 122 us -> 120 us (0.984)
  Pallas kernels: 117 us -> 115 us
    pallas_call x1, Pallas kernels: 117 us -> 115 us  [region(): pl.pallas_call(region_kernel, out_shape=jax.ShapeDtypeStruct((1, BLK), jn...]
where the time goes in v4:
time: 120 us; the launch traced here: 119 us
  Pallas kernels  115 us (96%)
  local copies, waits for them, and re-layouts  3.76 us (3%)
    pallas_call x1, Pallas kernels, region(): pl.pallas_call(region_kernel, out_shape=jax.ShapeDtypeStruct((1, BLK), jn...  115 us
    unnamed x2, local copies, waits for them, and re-layouts  2.41 us

profile of v4, /device:TPU:1, one launch (start us, length us, event | category | flops | bytes accessed | tf_op | source)
XLA Modules:
  0.0 119.4 jit_solution(16071379542406999867)
XLA Ops:
  0.7 1.3 %copy.12 = s32[1,1,3,6]{3,2,1,0:T(4,128)} copy(s32[1,1,3,6]{3,1,2,0:T(1,128)} %param.10) | data formatting | bytes 144
  1.9 1.4 %copy.9 = s32[1,16,3]{2,1,0:T(8,128)} copy(s32[1,16,3]{1,0,2:T(1,128)} %param.11) | data formatting | bytes 384 | tf_op jit(solution)/shard_map/squeeze | solution.py:474
  3.3 115.0 %region.1 = f32[1,128]{1,0:T(1,128)} custom-call(bf16[256,2048]{1,0:T(8,128)(2,1)} %bitcast.9, bf16[2,8,128,128]{3,2,1,0:T(8,128)(2,1)} %bitcast.10, s32[2,8]{1,0:T(2,128)} %bitcast.13, s32[3,6]{1,0:T(4,128)} %bitcast.12, s32[16,3]{1,0:T(8,128)} %bitcast.11, f32[1]{0:T(128)S(6)} %copy.14.mu_in, bf16[6,768,1536]{2,1,0:T(8,128)(2,1)} %bitcast.8), custom_call_target="tpu_custom_call" | custom-call | tf_op jit(solution)/shard_map/region/pallas_call | solution.py:444
  118.2 1.1 copy.15

commit v5 on v4

--- a/solution.py
+++ b/solution.py
@@ -140,13 +140,13 @@
         x_all[i, NZ] = jnp.zeros((BLK, BLK), jnp.bfloat16)
 
     def item_for(source, owner):
-        found = sum(k * (owners[source, k] == owner).astype(jnp.int32) for k in range(1, SUB_DEV))
+        found = sum(k * (owners[k, 0, source] == owner).astype(jnp.int32) for k in range(1, SUB_DEV))
         return jnp.minimum(found, SUB_DEV - 1)
 
     count = jnp.int32(0)
     slot_source = [jnp.int32(0)] * OWN_MAX
     for source in range(16):
-        has = sum((owners[source, k] == g).astype(jnp.int32) for k in range(SUB_DEV))
+        has = sum((owners[k, 0, source] == g).astype(jnp.int32) for k in range(SUB_DEV))
         has = jnp.minimum(has, 1)
         for t in range(OWN_MAX):
             slot_source[t] += source * has * (count == t).astype(jnp.int32)
@@ -189,7 +189,7 @@
 
     def pick_blocks(k, h_ref, chip, blocks):
         for b in range(SUB_BLK):
-            pick = picks[k, b]
+            pick = picks[k, 0, b]
             rows = slice(b * BLK, (b + 1) * BLK)
             for c in range(2):
                 for n, block in enumerate(blocks):
@@ -230,7 +230,7 @@
         if far == H_FAR_A:
             accumulate(ref, y_far, (0,), False)
 
-    mu = mu_in[0]
+    mu = mu_in[0, 0]
 
     class Way:
         def __init__(self, line, me, prev, nxt, swap_me, swap_prev, swap_nxt, x_first, bufs, base):
@@ -471,7 +471,8 @@
 
 def on_device(h_rows, x_blocks, x_cols, sub_blocks, owners, shift_mu, orbitals):
     return region(
-        h_rows[0], x_blocks[0], x_cols[0], sub_blocks[0, 0], owners[0], shift_mu, orbitals[0, 0]
+        h_rows[0], x_blocks[0], x_cols[0], jnp.transpose(sub_blocks[0], (1, 0, 2)),
+        jnp.transpose(owners, (2, 0, 1)), shift_mu.reshape(1, 1), orbitals[0, 0],
     )
 
 

time: 120 us -> 117 us (0.975)
  local copies, waits for them, and re-layouts: 3.76 us -> 1.19 us
    squeeze x1 -> x0, local copies, waits for them, and re-layouts: 1.35 us -> none  [on_device(): owners[0]]
    unnamed x2 -> x1, local copies, waits for them, and re-layouts: 2.41 us -> 1.19 us
where the time goes in v5:
time: 117 us
  Pallas kernels  115 us (98%)
  local copies, waits for them, and re-layouts  1.19 us (1%)
    pallas_call x1, Pallas kernels, region(): pl.pallas_call(region_kernel, out_shape=jax.ShapeDtypeStruct((1, BLK), jn...  115 us

profile of v5, /device:TPU:1, one launch (start us, length us, event | category | flops | bytes accessed | tf_op | source)
XLA Modules:
  0.0 117.0 jit_solution(12379535582596484611)
XLA Ops:
  0.7 115.1 %region.1 = f32[1,128]{1,0:T(1,128)} custom-call(bf16[256,2048]{1,0:T(8,128)(2,1)} %bitcast.9, bf16[2,8,128,128]{3,2,1,0:T(8,128)(2,1)} %bitcast.10, s32[2,8]{1,0:T(2,128)} %bitcast.13, s32[3,1,6]{2,1,0:T(1,128)} %bitcast.11, s32[3,1,16]{2,1,0:T(1,128)} %bitcast.12, f32[1,1]{1,0:T(1,128)} %bitcast.7.mu_in, bf16[6,768,1536]{2,1,0:T(8,128)(2,1)} %bitcast.8), custom_call_target="tpu_custom_call" | custom-call | tf_op jit(solution)/shard_map/region/pallas_call | solution.py:444
  115.8 1.2 %copy.10 = f32[1,128]{1,0:T(1,128)} copy(f32[1,128]{1,0:T(1,128)} %region.1) | data formatting | bytes 1024

commit v6 on v5

--- a/solution.py
+++ b/solution.py
@@ -335,6 +335,10 @@
             cols = slice(n * TILE, (n + 1) * TILE)
             step = jnp.dot(w[...], y0[:, cols], preferred_element_type=jnp.float32)
             z1[:, cols] = (scale_z * step).astype(jnp.bfloat16)
+        @pl.when(k > 0)
+        def _():
+            pass_on(k - 1)
+
         square = jnp.dot(z1[...], z1[:, :BLK], preferred_element_type=jnp.float32)
         eye = eye_like(ORDER, BLK, 0)
         y1[...] = (jnp.where(eye, 3.0, 0.0) - square).astype(jnp.bfloat16)
@@ -345,10 +349,6 @@
         for way in ways:
             way.line_copy(0, k).start()
             way.line_copy(1, k).start()
-
-        @pl.when(k > 0)
-        def _():
-            pass_on(k - 1)
 
         return carry
 

time: 117 us -> 121 us (1.034)
  Pallas kernels: 115 us -> 119 us
    pallas_call x1, Pallas kernels: 115 us -> 119 us  [region(): pl.pallas_call(region_kernel, out_shape=jax.ShapeDtypeStruct((1, BLK), jn...]
where the time goes in v6:
time: 121 us; the launch traced here: 120 us
  Pallas kernels  119 us (98%)
    pallas_call x1, Pallas kernels, region(): pl.pallas_call(region_kernel, out_shape=jax.ShapeDtypeStruct((1, BLK), jn...  119 us

profile of v6, /device:TPU:1, one launch (start us, length us, event | category | flops | bytes accessed | tf_op | source)
XLA Modules:
  0.0 120.5 jit_solution(4068838867636482037)
XLA Ops:
  0.7 118.6 %region.1 = f32[1,128]{1,0:T(1,128)} custom-call(bf16[256,2048]{1,0:T(8,128)(2,1)} %bitcast.9, bf16[2,8,128,128]{3,2,1,0:T(8,128)(2,1)} %bitcast.10, s32[2,8]{1,0:T(2,128)} %bitcast.13, s32[3,1,6]{2,1,0:T(1,128)} %bitcast.11, s32[3,1,16]{2,1,0:T(1,128)} %bitcast.12, f32[1,1]{1,0:T(1,128)} %bitcast.7.mu_in, bf16[6,768,1536]{2,1,0:T(8,128)(2,1)} %bitcast.8), custom_call_target="tpu_custom_call" | custom-call | tf_op jit(solution)/shard_map/region/pallas_call | solution.py:444
  119.3 1.2 copy.10
